TPU v7x, 32 devices: a whole 2x2x4 slice. The times are simulated.
32 devices in a mesh: azim: 8 (over z, x), frame: 4 (over y, core).
Axes of the slice: x: 2, y: 2, z: 4, core: 2. Of those that a mesh axis runs over, the one named last changes fastest.
Arguments:
- features: bfloat16 [4, 14, 112, 384], P('frame', None, 'azim'), may hold values from -6 to 6
- position_bias: float32 [169, 12], replicated, may hold values from -4 to 4
- attend_weight: bfloat16 [384, 1152], replicated, may hold values from -0.3125 to 0.3125
- output_weight: bfloat16 [384, 384], replicated, may hold values from -0.3125 to 0.3125
- merge_weight: bfloat16 [1536, 768], replicated, may hold values from -0.15625 to 0.15625
- cotangent: bfloat16 [4, 7, 56, 768], P('frame', None, 'azim'), may hold values from -6 to 6
Outputs:
- merged: bfloat16 [4, 7, 56, 768], P('frame', None, 'azim')
- feature_grad: bfloat16 [4, 14, 112, 384], P('frame', None, 'azim')
- attend_grad: float32 [442368], P(('azim', 'frame'))
- output_grad: float32 [147456], P(('azim', 'frame'))
All inputs are finite; a program needn't handle non-finite values.
Results may differ from a plain program's by a relative error of at most 0.0094.
Values may be sent and summed in bfloat16 or wider, within the bound.
No kernel may reach another device: no remote copies, remote signals or barrier semaphores. Data moves between devices by JAX's collectives and lax.ppermute only.
A program may use at most 64 MiB of HBM per device.

v0:
```python
import jax
import jax.numpy as jnp
from jax import lax
from jax.sharding import PartitionSpec as P


def from_behind(block, axis, distance):
    devices = range(lax.axis_size(axis))
    route = [((i - distance) % len(devices), i) for i in devices]
    return lax.ppermute(block, axis, route)


def to_windows(grid):
    row_count, col_count, channels = grid.shape
    grid = grid.reshape(row_count // 7, 7, col_count // 7, 7, channels).transpose(0, 2, 1, 3, 4)
    return grid.reshape(row_count // 7, col_count // 7, 49, channels)


def from_windows(blocks, row_count, col_count):
    channels = blocks.shape[-1]
    grid = blocks.reshape(row_count // 7, col_count // 7, 7, 7, channels).transpose(0, 2, 1, 3, 4)
    return grid.reshape(row_count, col_count, channels)


def normalize(values):
    centred = values - jnp.mean(values, -1, keepdims=True)
    inverse_std = lax.rsqrt(jnp.mean(centred * centred, -1, keepdims=True) + 1e-05)
    return (centred * inverse_std, inverse_std)


def normalize_back(normed, inverse_std, grads):
    first = jnp.mean(grads, -1, keepdims=True)
    second = jnp.mean(grads * normed, -1, keepdims=True)
    return inverse_std * (grads - first - normed * second)


def window_bias(position_bias, row_count):
    position = jnp.arange(49)
    pos_row = position // 7
    pos_col = position % 7
    bias_index = (pos_row[:, None] - pos_row[None, :] + 6) * 13 + (
        pos_col[:, None] - pos_col[None, :] + 6
    )
    one_hot = (bias_index.reshape(-1)[:, None] == jnp.arange(169)[None, :]).astype(
        position_bias.dtype
    )
    pos_bias = jnp.dot(one_hot, position_bias, precision=lax.Precision.HIGHEST)
    pos_bias = pos_bias.reshape(49, 49, -1).transpose(2, 0, 1)
    line_index = jnp.arange(row_count // 7)[:, None] * 7 + pos_row[None, :]
    region = (line_index >= row_count - 7).astype(jnp.int32) + (line_index >= row_count - 3).astype(
        jnp.int32
    )
    row_mask = jnp.where(region[:, :, None] == region[:, None, :], 0.0, -100.0).astype(
        position_bias.dtype
    )
    return (pos_bias, row_mask)


def merge_quads(grid):
    row_count, col_count, channels = grid.shape
    grid = grid.reshape(row_count // 2, 2, col_count // 2, 2, channels).transpose(0, 2, 3, 1, 4)
    return grid.reshape(row_count // 2, col_count // 2, 4 * channels)


def split_quads(grid, channels):
    half_rows, half_cols, _ = grid.shape
    grid = grid.reshape(half_rows, half_cols, 2, 2, channels).transpose(0, 3, 1, 2, 4)
    return grid.reshape(2 * half_rows, 2 * half_cols, channels)


def attention_forward(rolled, attend_weight, pos_bias, row_mask):
    row_count, col_count, channels = rolled.shape
    head_count = pos_bias.shape[0]
    head_size = channels // head_count
    projected = jnp.dot(
        rolled.reshape(-1, channels), attend_weight, preferred_element_type=jnp.float32
    )
    projected = projected.astype(jnp.bfloat16).reshape(row_count, col_count, 3 * channels)
    blocks = to_windows(projected)
    head_shape = blocks.shape[:3] + (head_count, head_size)
    queries = blocks[..., :channels].reshape(head_shape)
    key_block = blocks[..., channels : 2 * channels].reshape(head_shape)
    value_block = blocks[..., 2 * channels :].reshape(head_shape)
    scores = jnp.einsum(
        "abqhd,abkhd->abhqk", queries, key_block, preferred_element_type=jnp.float32
    ) * head_size ** (-0.5)
    scores = scores + pos_bias[None, None] + row_mask[:, None, None]
    probs = jax.nn.softmax(scores, -1)
    probs16 = probs.astype(jnp.bfloat16)
    attended = jnp.einsum(
        "abhqk,abkhd->abqhd", probs16, value_block, preferred_element_type=jnp.float32
    )
    attended = attended.astype(jnp.bfloat16).reshape(head_shape[:3] + (channels,))
    return (
        from_windows(attended, row_count, col_count),
        (queries, key_block, value_block, probs, probs16),
    )


def attention_backward(attended_grad, saved, head_size):
    queries, key_block, value_block, probs, probs16 = saved
    row_count, col_count, channels = attended_grad.shape
    outer = to_windows(attended_grad).reshape(queries.shape)
    value_grad = jnp.einsum(
        "abhqk,abqhd->abkhd", probs16, outer, preferred_element_type=jnp.float32
    )
    score_grad = jnp.einsum(
        "abqhd,abkhd->abhqk", outer, value_block, preferred_element_type=jnp.float32
    )
    soft_grad = (
        probs * (score_grad - jnp.sum(probs * score_grad, -1, keepdims=True)) * head_size ** (-0.5)
    )
    soft16 = soft_grad.astype(jnp.bfloat16)
    query_grad = jnp.einsum(
        "abhqk,abkhd->abqhd", soft16, key_block, preferred_element_type=jnp.float32
    )
    key_grad = jnp.einsum("abhqk,abqhd->abkhd", soft16, queries, preferred_element_type=jnp.float32)
    flat_shape = queries.shape[:3] + (channels,)
    joined = jnp.concatenate(
        [
            query_grad.reshape(flat_shape),
            key_grad.reshape(flat_shape),
            value_grad.reshape(flat_shape),
        ],
        -1,
    )
    return from_windows(joined.astype(jnp.bfloat16), row_count, col_count)


def token_product(left, right):
    return lax.dot_general(
        left.reshape(-1, left.shape[-1]),
        right.reshape(-1, right.shape[-1]),
        (((0,), (0,)), ((), ())),
        preferred_element_type=jnp.float32,
    )


def per_device(features, position_bias, attend_weight, output_weight, merge_weight, cotangent):
    local_frame = features[0]
    row_count, col_count, channels = local_frame.shape
    head_size = channels // position_bias.shape[1]
    pos_bias, row_mask = window_bias(position_bias, row_count)
    east_cols = from_behind(local_frame[:, :3], "azim", -1)
    extended = jnp.concatenate([local_frame[:, 3:], east_cols], 1)
    normed, inverse_std = normalize(extended.astype(jnp.float32))
    normed = jnp.roll(normed, -3, 0)
    inverse_std = jnp.roll(inverse_std, -3, 0)
    rolled = normed.astype(jnp.bfloat16)
    attended, saved = attention_forward(rolled, attend_weight, pos_bias, row_mask)
    branch = jnp.dot(
        attended.reshape(-1, channels), output_weight, preferred_element_type=jnp.float32
    )
    branch = jnp.roll(branch.reshape(row_count, col_count, channels), 3, 0)
    west_part = from_behind(branch[:, col_count - 3 :].astype(jnp.bfloat16), "azim", 1).astype(
        jnp.float32
    )
    branch_own = jnp.concatenate([west_part, branch[:, : col_count - 3]], 1)
    hidden = (local_frame.astype(jnp.float32) + branch_own).astype(jnp.bfloat16)
    quad_normed, quad_std = normalize(merge_quads(hidden).astype(jnp.float32))
    quad16 = quad_normed.astype(jnp.bfloat16)
    out_width = merge_weight.shape[1]
    merged = jnp.dot(
        quad16.reshape(-1, 4 * channels), merge_weight, preferred_element_type=jnp.float32
    )
    merged = merged.astype(jnp.bfloat16).reshape(row_count // 2, col_count // 2, out_width)
    quad_grad_in = jnp.dot(
        cotangent[0].reshape(-1, out_width), merge_weight.T, preferred_element_type=jnp.float32
    )
    quad_grad = normalize_back(quad_normed, quad_std, quad_grad_in.reshape(quad_normed.shape))
    hidden_grad = split_quads(quad_grad, channels).astype(jnp.bfloat16)
    east_grads = from_behind(hidden_grad[:, :3], "azim", -1)
    branch_grad = jnp.roll(jnp.concatenate([hidden_grad[:, 3:], east_grads], 1), -3, 0)
    output_part = token_product(attended, branch_grad)
    attended_grad = jnp.dot(
        branch_grad.reshape(-1, channels), output_weight.T, preferred_element_type=jnp.float32
    )
    attended_grad = attended_grad.astype(jnp.bfloat16).reshape(row_count, col_count, channels)
    projected_grad = attention_backward(attended_grad, saved, head_size)
    attend_part = token_product(rolled, projected_grad)
    normed_grad = jnp.dot(
        projected_grad.reshape(-1, 3 * channels),
        attend_weight.T,
        preferred_element_type=jnp.float32,
    )
    rolled_grad = normalize_back(
        normed, inverse_std, normed_grad.reshape(row_count, col_count, channels)
    )
    rolled_grad = jnp.roll(rolled_grad, 3, 0)
    west_grads = from_behind(
        rolled_grad[:, col_count - 3 :].astype(jnp.bfloat16), "azim", 1
    ).astype(jnp.float32)
    rolled_own = jnp.concatenate([west_grads, rolled_grad[:, : col_count - 3]], 1)
    feature_grad = (hidden_grad.astype(jnp.float32) + rolled_own).astype(jnp.bfloat16)
    flat_terms = (attend_part.reshape(-1), output_part.reshape(-1))
    attend_total, output_total = lax.psum((flat_terms[0], flat_terms[1]), ("azim", "frame"))
    members = lax.axis_size(("azim", "frame"))
    position = lax.axis_index(("azim", "frame"))
    attend_count = attend_total.shape[0] // members
    output_count = output_total.shape[0] // members
    attend_grad = lax.dynamic_slice_in_dim(attend_total, position * attend_count, attend_count)
    output_grad = lax.dynamic_slice_in_dim(output_total, position * output_count, output_count)
    return (merged[None], feature_grad[None], attend_grad, output_grad)


def solution(mesh):
    in_specs = (P("frame", None, "azim", None), P(), P(), P(), P(), P("frame", None, "azim", None))
    out_specs = (
        P("frame", None, "azim", None),
        P("frame", None, "azim", None),
        P(("azim", "frame")),
        P(("azim", "frame")),
    )
    return jax.shard_map(
        per_device, mesh=mesh, in_specs=in_specs, out_specs=out_specs, check_vma=False
    )
```

profile of v0, /device:TPU:0, one launch (start us, length us, event | category | flops | bytes accessed | tf_op | source)
XLA Modules:
  0.0 249.8 jit_solution(12866885575160851997)
XLA Ops:
  7.2 1.7 slice.111
  8.9 6.0 %collective-permute-start = (bf16[14,3,384]{2,1,0:T(4,128)(2,1)}, bf16[14,3,384]{2,1,0:T(4,128)(2,1)S(1)}, u32[]{:S(2)}, u32[]{:S(2)}) collective-permute-start(bf16[14,3,384]{2,1,0:T(4,128)(2,1)} %slice.111), channel_id=1, source_target_pairs={{4,0},{8,4},{12,8},{16,12},{20,16},{24,20},{28,24},{0,28},{5,1},{9... | collective-permute-start | bytes 96776 | tf_op jit(solution)/shard_map/ppermute | solution.py:10
  15.2 2.0 fusion.2
  17.9 1.0 slice.110
  18.9 1.8 reshape.358
  20.9 0.9 copy.24
  23.7 1.6 convert_element_type.156
  25.3 2.1 convolution_convert_fusion
  27.4 1.2 reshape_reshape.20
  29.5 1.0 copy.22
  30.5 1.0 copy.23
  31.5 3.1 %fusion.68 = (f32[2,2,12,49]{3,2,1,0:T(8,128)S(1)}, f32[2,2,12,49,49]{3,4,2,1,0:T(8,128)}) fusion(bf16[2,2,49,12,32]{2,4,3,1,0:T(8,128)(2,1)} %bitcast.98, bf16[2,2,49,12,32]{2,4,3,1,0:T(8,128)(2,1)} %bitcast.100, f32[2,49,49]{1,2,0:T(8,128)} %compare_select_fusion, f32[12,49,49]{1,2,0:T(8,128)} %bitcast.102), kind=kOutput, calls=%fused_computation.112 | convolution fusion | flops 7952160 | bytes 905912 | tf_op jit(solution)/shard_map/sub | solution.py:88
  35.3 2.4 fusion.33
  37.7 2.4 copy.26
  40.1 1.4 reshape_reshape.21
  41.4 0.9 copy.27
  42.4 1.3 fusion.69
  45.2 0.9 slice.148
  46.2 6.7 %collective-permute-done.1 = bf16[14,3,384]{2,1,0:T(4,128)(2,1)S(1)} collective-permute-done((bf16[14,3,384]{2,1,0:T(4,128)(2,1)S(1)}, bf16[14,3,384]{2,1,0:T(4,128)(2,1)S(1)}, u32[]{:S(2)}, u32[]{:S(2)}) %collective-permute-start.1) | collective-permute-done | bytes 32288 | tf_op jit(solution)/shard_map/ppermute | solution.py:10
  52.9 1.0 pad_maximum_fusion.2
  54.2 1.4 fusion.51
  56.2 1.0 reshape.359
  57.5 1.0 fusion.65
  58.9 0.9 copy_bitcast_fusion
  60.7 1.2 convolution_convert_fusion.4
  61.9 1.6 broadcast_in_dim_reshape.4
  63.5 1.9 reshape.361
  67.0 1.7 reshape_reshape.24
  68.7 1.5 copy.32
  70.3 2.8 %fusion.34 = bf16[2,2,49,12,32]{2,4,3,1,0:T(8,128)(2,1)} fusion(bf16[2,2,49,12,32]{2,4,3,1,0:T(8,128)(2,1)} %copy.32, f32[2,2,12,49,49]{3,4,2,1,0:T(8,128)} %get-tuple-element.18, f32[2,2,12,49]{3,2,1,0:T(8,128)S(1)} %copy-done.21), kind=kOutput, calls=%fused_computation.28 | convolution fusion | flops 7681632 | bytes 771456 | tf_op jit(solution)/shard_map/abhqk,abqhd->abkhd/dot_general | solution.py:104
  73.0 1.7 fusion.70
  74.7 4.0 %fusion.27 = bf16[2,2,49,12,32]{2,4,3,1,0:T(8,128)(2,1)} fusion(bf16[2,2,49,12,32]{2,4,3,1,0:T(8,128)(2,1)S(1)} %bitcast.99, f32[2,2,12,49,49]{3,4,2,1,0:T(8,128)} %fusion.70, f32[2,2,12,49,49]{3,4,2,1,0:T(8,128)} %get-tuple-element.18, f32[2,2,12,49]{3,2,1,0:T(8,128)S(1)} %copy-done.21), kind=kOutput, calls=%fused_computation.25 | convolution fusion | flops 8260272 | bytes 1232448 | tf_op jit(solution)/shard_map/abhqk,abqhd->abkhd/dot_general | solution.py:117
  78.7 4.0 %fusion.30 = bf16[2,2,49,12,32]{2,4,3,1,0:T(8,128)(2,1)} fusion(bf16[2,2,49,12,32]{2,4,3,1,0:T(8,128)(2,1)S(1)} %bitcast.101, f32[2,2,12,49,49]{3,4,2,1,0:T(8,128)} %fusion.70, f32[2,2,12,49,49]{3,4,2,1,0:T(8,128)} %get-tuple-element.18, f32[2,2,12,49]{3,2,1,0:T(8,128)S(1)} %copy-done.21), kind=kOutput, calls=%fused_computation.26 | convolution fusion | flops 8260272 | bytes 1232448 | tf_op jit(solution)/shard_map/abhqk,abkhd->abqhd/dot_general | solution.py:114
  82.7 2.4 copy.39
  85.1 1.4 concatenate.67
  86.4 2.4 copy.36
  88.8 1.4 concatenate.66
  90.2 2.4 copy.34
  92.6 1.4 concatenate.65
  93.9 1.5 maximum_bitcast_fusion
  97.6 2.5 %fusion.64 = (f32[14,14]{1,0:T(8,128)S(1)}, f32[14,14]{1,0:T(8,128)S(1)}, f32[14,14,384]{2,1,0:T(8,128)}) fusion(f32[3,14,384]{2,1,0:T(8,128)} %copy-done.14, f32[11,14,384]{2,1,0:T(8,128)S(1)} %slice.112, bf16[14,14,1152]{2,1,0:T(8,128)(2,1)} %dot_general.62, bf16[384,1152]{1,0:T(8,128)(2,1)} %param.8), kind=kOutput, calls=%fused_computation.109 | convolution fusion | flops 173708928 | bytes 1940000 | tf_op jit(solution)/shard_map/dot_general | solution.py:181
  100.1 1.7 fusion.71
  101.8 2.5 %reshape.356 = f32[442368]{0:T(1024)} reshape(f32[384,1152]{1,0:T(8,128)} %fusion.71) | data formatting | bytes 3538944 | tf_op jit(solution)/shard_map/reshape | solution.py:195
  106.4 2.1 collective-permute-start.3
  108.5 4.8 %collective-permute-done.3 = bf16[14,3,384]{2,1,0:T(4,128)(2,1)S(1)} collective-permute-done((bf16[14,3,384]{2,1,0:T(4,128)(2,1)S(1)}, bf16[14,3,384]{2,1,0:T(4,128)(2,1)S(1)}, u32[]{:S(2)}, u32[]{:S(2)}) %collective-permute-start.3) | collective-permute-done | bytes 32288 | tf_op jit(solution)/shard_map/ppermute | solution.py:10
  114.1 125.9 %all-reduce.3.cloned.1.call-done = (f32[442368]{0:T(1024)}, f32[147456]{0:T(1024)}) async-done(((f32[442368]{0:T(1024)}, f32[147456]{0:T(1024)}), (f32[442368]{0:T(1024)}, f32[147456]{0:T(1024)})) %all-reduce.3.cloned.1.call-update) | async-done | bytes 2359312 | tf_op jit(solution)/shard_map/psum | solution.py:196
  240.0 1.5 dynamic_slice.6
  241.6 1.4 dynamic_slice.7
  (114 shorter events, 15.1 us)
Async XLA Ops:
  7.2 50.3 %copy-start = (bf16[1536,768]{1,0:T(8,128)(2,1)S(1)}, bf16[1536,768]{1,0:T(8,128)(2,1)}, u32[]{:S(2)}) copy-start(bf16[1536,768]{1,0:T(8,128)(2,1)} %param.10) | copy-start | bytes 7077892
  7.2 232.8 %all-reduce.3.cloned.1.call-start = ((), (), s32[]{:S(2)}) async-start(), calls=%async_computation | async-start | bytes 4718592 | tf_op jit(solution)/shard_map/psum | solution.py:196
  8.9 12.9 %collective-permute-start = (bf16[14,3,384]{2,1,0:T(4,128)(2,1)}, bf16[14,3,384]{2,1,0:T(4,128)(2,1)S(1)}, u32[]{:S(2)}, u32[]{:S(2)}) collective-permute-start(bf16[14,3,384]{2,1,0:T(4,128)(2,1)} %slice.111), channel_id=1, source_target_pairs={{4,0},{8,4},{12,8},{16,12},{20,16},{24,20},{28,24},{0,28},{5,1},{9... | collective-permute-start | bytes 96776 | tf_op jit(solution)/shard_map/ppermute | solution.py:10
  21.8 3.5 %copy-start.1 = (bf16[384,1152]{1,0:T(8,128)(2,1)S(1)}, bf16[384,1152]{1,0:T(8,128)(2,1)}, u32[]{:S(2)}) copy-start(bf16[384,1152]{1,0:T(8,128)(2,1)} %param.8) | copy-start | bytes 2654212
  22.3 0.6 copy-start.14
  29.5 5.1 %copy-start.3 = (bf16[2,2,49,384]{2,3,1,0:T(8,128)(2,1)}, bf16[2,2,49,384]{2,3,1,0:T(8,128)(2,1)S(1)}, u32[]{:S(2)}) copy-start(bf16[2,2,49,384]{2,3,1,0:T(8,128)(2,1)S(1)} %copy.21) | copy-start | bytes 451588
  34.6 0.6 copy-start.20
  42.4 2.8 %copy-start.6 = (bf16[196,384]{1,0:T(8,128)(2,1)}, bf16[196,384]{1,0:T(8,128)(2,1)S(1)}, u32[]{:S(2)}) copy-start(bf16[196,384]{1,0:T(8,128)(2,1)S(1)} %reshape_reshape.22) | copy-start | bytes 451588
  46.2 6.8 %collective-permute-start.1 = (bf16[14,3,384]{2,1,0:T(4,128)(2,1)S(1)}, bf16[14,3,384]{2,1,0:T(4,128)(2,1)S(1)}, u32[]{:S(2)}, u32[]{:S(2)}) collective-permute-start(bf16[14,3,384]{2,1,0:T(4,128)(2,1)S(1)} %slice.148), channel_id=1, source_target_pairs={{28,0},{0,4},{4,8},{8,12},{12,16},{16,20},{20,24},{24,28},{29,1},{... | collective-permute-start | bytes 96776 | tf_op jit(solution)/shard_map/ppermute | solution.py:10
  54.2 3.3 %copy-start.19 = (bf16[1,7,7,768]{3,2,1,0:T(8,128)(2,1)S(1)}, bf16[1,7,7,768]{3,2,1,0:T(8,128)(2,1)}, u32[]{:S(2)}) copy-start(bf16[1,7,7,768]{3,2,1,0:T(8,128)(2,1)} %param.11) | copy-start | bytes 225796
  58.5 2.2 copy-start.11
  60.7 4.8 %collective-permute-start.2 = (bf16[14,3,384]{2,1,0:T(4,128)(2,1)}, bf16[14,3,384]{2,1,0:T(4,128)(2,1)S(1)}, u32[]{:S(2)}, u32[]{:S(2)}) collective-permute-start(bf16[14,3,384]{2,1,0:T(4,128)(2,1)} %slice.124), channel_id=1, source_target_pairs={{4,0},{8,4},{12,8},{16,12},{20,16},{24,20},{28,24},{0,28},{5,1},{9... | collective-permute-start | bytes 96776 | tf_op jit(solution)/shard_map/ppermute | solution.py:10
  61.9 3.7 %copy-start.16 = (bf16[384,384]{1,0:T(8,128)(2,1)S(1)}, bf16[384,384]{1,0:T(8,128)(2,1)}, u32[]{:S(2)}) copy-start(bf16[384,384]{1,0:T(8,128)(2,1)} %param.9) | copy-start | bytes 884740
  65.6 0.7 copy-start.8
  65.9 4.3 %copy-start.21 = (f32[2,2,12,49]{3,2,1,0:T(8,128)S(1)}, f32[2,2,12,49]{3,2,1,0:T(8,128)}, u32[]{:S(2)}) copy-start(f32[2,2,12,49]{3,2,1,0:T(8,128)} %copy-done.20) | copy-start | bytes 28228
  70.2 2.8 %copy-start.4 = (bf16[2,2,49,384]{2,3,1,0:T(8,128)(2,1)S(1)}, bf16[2,2,49,384]{2,3,1,0:T(8,128)(2,1)}, u32[]{:S(2)}) copy-start(bf16[2,2,49,384]{2,3,1,0:T(8,128)(2,1)} %copy-done.3) | copy-start | bytes 451588
  70.2 2.8 %copy-start.5 = (bf16[2,2,49,12,32]{2,4,3,1,0:T(8,128)(2,1)S(1)}, bf16[2,2,49,12,32]{2,4,3,1,0:T(8,128)(2,1)}, u32[]{:S(2)}) copy-start(bf16[2,2,49,12,32]{2,4,3,1,0:T(8,128)(2,1)} %copy.32) | copy-start | bytes 451588
  73.0 1.7 copy-start.17
  74.7 4.0 %copy-start.18 = (bf16[2,2,49,384]{2,3,1,0:T(8,128)(2,1)S(1)}, bf16[2,2,49,384]{2,3,1,0:T(8,128)(2,1)}, u32[]{:S(2)}) copy-start(bf16[2,2,49,384]{2,3,1,0:T(8,128)(2,1)} %copy.23) | copy-start | bytes 451588
  95.4 1.9 copy-start.7
  95.4 1.9 copy-start.9
  97.3 2.8 %copy-start.2 = (bf16[196,1152]{1,0:T(8,128)(2,1)S(1)}, bf16[196,1152]{1,0:T(8,128)(2,1)}, u32[]{:S(2)}) copy-start(bf16[196,1152]{1,0:T(8,128)(2,1)} %reshape_reshape.25) | copy-start | bytes 1354756
  97.3 2.8 %copy-start.10 = (bf16[196,384]{1,0:T(8,128)(2,1)S(1)}, bf16[196,384]{1,0:T(8,128)(2,1)}, u32[]{:S(2)}) copy-start(bf16[196,384]{1,0:T(8,128)(2,1)} %convert_element_type.156) | copy-start | bytes 451588
  105.2 1.0 copy-start.13
  105.2 1.0 copy-start.15
  106.2 7.2 %copy-start.12 = (f32[1,14,14,384]{3,2,1,0:T(8,128)S(1)}, f32[1,14,14,384]{3,2,1,0:T(8,128)}, u32[]{:S(2)}) copy-start(f32[1,14,14,384]{3,2,1,0:T(8,128)} %reshape.361) | copy-start | bytes 903172
  106.4 6.9 %collective-permute-start.3 = (bf16[14,3,384]{2,1,0:T(4,128)(2,1)S(1)}, bf16[14,3,384]{2,1,0:T(4,128)(2,1)S(1)}, u32[]{:S(2)}, u32[]{:S(2)}) collective-permute-start(bf16[14,3,384]{2,1,0:T(4,128)(2,1)S(1)} %fusion.54), channel_id=1, source_target_pairs={{28,0},{0,4},{4,8},{8,12},{12,16},{16,20},{20,24},{24,28},{29,1},{... | collective-permute-start | bytes 96776 | tf_op jit(solution)/shard_map/ppermute | solution.py:10
Sparse Core Ops, SparseCore 0:
  105.3 134.6 all-reduce.2
where the time goes:
time: 251 us; the launch traced here: 250 us
  waiting for transfers between devices  137 us (55%)
  local copies, waits for them, and re-layouts  50.8 us (20%)
  matrix products  30.3 us (12%)
  between operations  14.5 us (6%)
  other arithmetic  8.61 us (3%)
  starting transfers between devices  8.18 us (3%)
    psum x1, waiting for transfers between devices, per_device(): lax.psum((flat_terms[0], flat_terms[1]), ('azim', 'frame'))  126 us
    ppermute x4, waiting for transfers between devices, from_behind(): return lax.ppermute(block, axis, route)  11.5 us
    ppermute x4, starting transfers between devices, from_behind(): return lax.ppermute(block, axis, route)  8.15 us
  transfers between devices with their start and end apart: 5, of which 3 were waited for; matrix products, arithmetic and copies ran while one was open for 5% of the time, Pallas kernels for 0%

commit v1 on v0

--- a/solution.py
+++ b/solution.py
@@ -136,6 +136,34 @@
     )
 
 
+def halving_bits():
+    frame_bits = lax.axis_size("frame").bit_length() - 1
+    azim_bits = lax.axis_size("azim").bit_length() - 1
+    bits = [("frame", bit, azim_bits + frame_bits - 1 - bit) for bit in range(frame_bits)]
+    bits += [("azim", bit, azim_bits - 1 - bit) for bit in range(azim_bits)]
+    order = [bits[0], bits[frame_bits]] + bits[1:frame_bits] + bits[frame_bits + 1 :][::-1]
+    return order, azim_bits + frame_bits
+
+
+def scatter_sum(terms):
+    members = lax.axis_size(("azim", "frame"))
+    widths = [term.size // members for term in terms]
+    order, bit_count = halving_bits()
+    joined = jnp.concatenate([term.reshape(members, -1) for term in terms], 1)
+    held = joined.astype(jnp.bfloat16).reshape((2,) * bit_count + (-1,))
+    for axis, bit, dim in order:
+        size = lax.axis_size(axis)
+        own = (lax.axis_index(axis) >> bit) & 1
+        route = [(i, i ^ (1 << bit)) for i in range(size)]
+        kept = lax.dynamic_slice_in_dim(held, own, 1, dim)
+        sent = lax.dynamic_slice_in_dim(held, 1 - own, 1, dim)
+        got = lax.ppermute(sent, axis, route)
+        total = kept.astype(jnp.float32) + got.astype(jnp.float32)
+        held = total.astype(jnp.bfloat16)
+    total = total.reshape(-1)
+    return total[: widths[0]], total[widths[0] :]
+
+
 def per_device(features, position_bias, attend_weight, output_weight, merge_weight, cotangent):
     local_frame = features[0]
     row_count, col_count, channels = local_frame.shape
@@ -192,14 +220,7 @@
     ).astype(jnp.float32)
     rolled_own = jnp.concatenate([west_grads, rolled_grad[:, : col_count - 3]], 1)
     feature_grad = (hidden_grad.astype(jnp.float32) + rolled_own).astype(jnp.bfloat16)
-    flat_terms = (attend_part.reshape(-1), output_part.reshape(-1))
-    attend_total, output_total = lax.psum((flat_terms[0], flat_terms[1]), ("azim", "frame"))
-    members = lax.axis_size(("azim", "frame"))
-    position = lax.axis_index(("azim", "frame"))
-    attend_count = attend_total.shape[0] // members
-    output_count = output_total.shape[0] // members
-    attend_grad = lax.dynamic_slice_in_dim(attend_total, position * attend_count, attend_count)
-    output_grad = lax.dynamic_slice_in_dim(output_total, position * output_count, output_count)
+    attend_grad, output_grad = scatter_sum((attend_part, output_part))
     return (merged[None], feature_grad[None], attend_grad, output_grad)
 
 

time: 251 us -> 141 us (0.56)
  waiting for transfers between devices: 137 us -> 35.6 us
  between operations: 14.5 us -> 1.27 us
  other arithmetic: 8.61 us -> 11.8 us
    psum x1 -> x0, waiting for transfers between devices: 126 us -> none  [per_device(): lax.psum((flat_terms[0], flat_terms[1]), ('azim', 'frame'))]
    ppermute x0 -> x5, waiting for transfers between devices: none -> 27.3 us  [scatter_sum(): got = lax.ppermute(sent, axis, route)]
    concatenate x0 -> x3, local copies, waits for them, and re-layouts: none -> 4.04 us  [scatter_sum(): joined = jnp.concatenate([term.reshape(members, -1) for term in terms], 1)]
    reshape x2 -> x0, local copies, waits for them, and re-layouts: 3.38 us -> none  [per_device(): flat_terms = (attend_part.reshape(-1), output_part.reshape(-1))]
    ppermute x4, waiting for transfers between devices: 11.5 us -> 8.31 us  [from_behind(): return lax.ppermute(block, axis, route)]
    convert_element_type x0 -> x4, other arithmetic: none -> 2.65 us  [scatter_sum(): held = total.astype(jnp.bfloat16)]
  transfers between devices with their start and end apart: 5 -> 9, of which waited for: 3 -> 6; matrix products, arithmetic and copies ran while one was open for 5% -> 11% of each run, Pallas kernels for 0% -> 0%
where the time goes in v1:
time: 141 us; the launch traced here: 140 us
  local copies, waits for them, and re-layouts  52.1 us (37%)
  waiting for transfers between devices  35.6 us (25%)
  matrix products  30.6 us (22%)
  other arithmetic  11.8 us (8%)
  starting transfers between devices  8.56 us (6%)
    ppermute x5, waiting for transfers between devices, scatter_sum(): got = lax.ppermute(sent, axis, route)  27.3 us
    ppermute x4, waiting for transfers between devices, from_behind(): return lax.ppermute(block, axis, route)  8.31 us
    ppermute x4, starting transfers between devices, from_behind(): return lax.ppermute(block, axis, route)  6.64 us
    unnamed x46, local copies, waits for them, and re-layouts  4.59 us
    concatenate x3, local copies, waits for them, and re-layouts, attention_backward(): jnp.concatenate([query_grad.reshape(flat_shape), key_grad.reshape(flat_sh...  4.09 us
    concatenate x3, local copies, waits for them, and re-layouts, scatter_sum(): joined = jnp.concatenate([term.reshape(members, -1) for term in terms], 1)  4.04 us
    dot_general x1, matrix products, attention_backward(): jnp.einsum('abhqk,abkhd->abqhd', soft16, key_block, preferred_element_typ...  4.01 us
    dot_general x1, matrix products, attention_backward(): jnp.einsum('abhqk,abqhd->abkhd', soft16, queries, preferred_element_type=...  3.99 us
  transfers between devices with their start and end apart: 9, of which 6 were waited for; matrix products, arithmetic and copies ran while one was open for 11% of the time, Pallas kernels for 0%

profile of v1, /device:TPU:0, one launch (start us, length us, event | category | flops | bytes accessed | tf_op | source)
XLA Modules:
  0.0 140.0 jit_solution(6689487289641017514)
XLA Ops:
  0.7 1.7 %slice.127 = bf16[14,3,384]{2,1,0:T(4,128)(2,1)} slice(bf16[14,14,384]{2,1,0:T(8,128)(2,1)} %bitcast.93), slice={[0:14], [0:3], [0:384]} | slice | bytes 64512 | tf_op jit(solution)/shard_map/slice | solution.py:172
  2.3 6.0 %collective-permute-start = (bf16[14,3,384]{2,1,0:T(4,128)(2,1)}, bf16[14,3,384]{2,1,0:T(4,128)(2,1)S(1)}, u32[]{:S(2)}, u32[]{:S(2)}) collective-permute-start(bf16[14,3,384]{2,1,0:T(4,128)(2,1)} %slice.127), channel_id=1, source_target_pairs={{4,0},{8,4},{12,8},{16,12},{20,16},{24,20},{28,24},{0,28},{5,1},{9... | collective-permute-start | bytes 96776 | tf_op jit(solution)/shard_map/ppermute | solution.py:10
  8.6 2.0 %fusion.2 = f32[2401,12]{0,1:T(8,128)S(1)} fusion(f32[169,12]{0,1:T(8,128)} %param.7, s32[2401]{0:T(1024)S(1)} %add.196), kind=kOutput, calls=%fused_computation.5 | convolution fusion | flops 58836504 | bytes 132964 | tf_op jit(solution)/shard_map/dot_general | solution.py:47
  11.3 1.0 slice.126
  16.2 1.6 %convert_element_type.200 = bf16[196,384]{1,0:T(8,128)(2,1)} reshape(bf16[14,14,384]{2,1,0:T(8,128)(2,1)} %fusion.47) | data formatting | bytes 301056 | tf_op jit(solution)/shard_map/convert_element_type | solution.py:177
  17.8 2.1 %convolution_convert_fusion.1 = bf16[196,1152]{1,0:T(8,128)(2,1)} fusion(bf16[196,384]{1,0:T(8,128)(2,1)} %convert_element_type.200, bf16[384,1152]{1,0:T(8,128)(2,1)S(1)} %copy-done.3), kind=kOutput, calls=%fused_computation.3 | convolution fusion | flops 173634048 | bytes 1486848 | tf_op jit(solution)/shard_map/dot_general | solution.py:75
  19.9 1.2 reshape_reshape.20
  21.8 1.0 copy.45
  22.8 1.0 copy.44
  24.1 3.2 %fusion.68 = (f32[2,2,12,49]{3,2,1,0:T(8,128)S(1)}, f32[2,2,12,49,49]{3,4,2,1,0:T(8,128)}) fusion(bf16[2,2,49,12,32]{2,4,3,1,0:T(8,128)(2,1)} %bitcast.100, bf16[2,2,49,12,32]{2,4,3,1,0:T(8,128)(2,1)} %bitcast.98, f32[2,49,49]{1,2,0:T(8,128)} %compare_select_fusion, f32[12,49,49]{1,2,0:T(8,128)S(1)} %bitcast.102), kind=kOutput, calls=%fused_computation.128 | convolution fusion | flops 7952160 | bytes 905912 | tf_op jit(solution)/shard_map/sub | solution.py:88
  27.9 2.4 %fusion.33 = bf16[2,2,49,12,32]{2,4,3,1,0:T(8,128)(2,1)} fusion(bf16[2,2,49,12,32]{2,4,3,1,0:T(8,128)(2,1)S(1)} %bitcast.91, f32[2,2,12,49,49]{3,4,2,1,0:T(8,128)} %get-tuple-element.16, f32[2,2,12,49]{3,2,1,0:T(8,128)S(1)} %get-tuple-element.15), kind=kOutput, calls=%fused_computation.29 | convolution fusion | flops 7681632 | bytes 771456 | tf_op jit(solution)/shard_map/abhqk,abkhd->abqhd/dot_general | solution.py:90
  30.3 2.4 %copy.48 = bf16[2,2,49,12,32]{4,3,1,2,0:T(8,128)(2,1)S(1)} copy(bf16[2,2,49,12,32]{2,4,3,1,0:T(8,128)(2,1)} %fusion.33) | data formatting | bytes 301056 | tf_op jit(solution)/shard_map/convert_element_type | solution.py:93
  32.7 1.4 reshape_reshape.21
  35.1 1.2 fusion.69
  36.5 6.7 %collective-permute-done.1 = bf16[14,3,384]{2,1,0:T(4,128)(2,1)S(1)} collective-permute-done((bf16[14,3,384]{2,1,0:T(4,128)(2,1)S(1)}, bf16[14,3,384]{2,1,0:T(4,128)(2,1)S(1)}, u32[]{:S(2)}, u32[]{:S(2)}) %collective-permute-start.1) | collective-permute-done | bytes 32288 | tf_op jit(solution)/shard_map/ppermute | solution.py:10
  44.2 1.4 %fusion.51 = (f32[7,7]{1,0:T(8,128)S(1)}, bf16[7,2,7,2,384]{4,1,3,2,0:T(2,128)(2,1)S(1)}) fusion(f32[7,2,7,2,384]{4,3,2,1,0:T(2,128)} %concatenate.70, f32[7,2,7,2,384]{4,3,2,1,0:T(2,128)} %reshape.362), kind=kLoop, calls=%fused_computation.77 | loop fusion | flops 301007 | bytes 752836 | tf_op jit(solution)/shard_map/reduce_sum | solution.py:26
  48.3 1.1 convert_element_type.218
  51.3 1.0 reshape.363
  52.3 1.0 slice.139
  53.2 1.6 %collective-permute-done.2 = bf16[14,3,384]{2,1,0:T(4,128)(2,1)S(1)} collective-permute-done((bf16[14,3,384]{2,1,0:T(4,128)(2,1)S(1)}, bf16[14,3,384]{2,1,0:T(4,128)(2,1)S(1)}, u32[]{:S(2)}, u32[]{:S(2)}) %collective-permute-start.2) | collective-permute-done | bytes 32288 | tf_op jit(solution)/shard_map/ppermute | solution.py:10
  55.6 1.0 reshape.361
  56.6 1.0 convolution_convert_fusion.4
  58.8 1.7 %reshape_reshape.24 = bf16[2,2,49,12,32]{4,3,1,2,0:T(8,128)(2,1)S(1)} reshape(bf16[2,2,7,7,384]{4,1,3,2,0:T(2,128)(2,1)} %copy.53) | data formatting | bytes 301056 | tf_op jit(solution)/shard_map/reshape;reshape | solution.py:103
  60.4 1.5 %copy.54 = bf16[2,2,49,12,32]{2,4,3,1,0:T(8,128)(2,1)} copy(bf16[2,2,49,12,32]{4,3,1,2,0:T(8,128)(2,1)S(1)} %reshape_reshape.24) | data formatting | bytes 301056 | tf_op jit(solution)/shard_map/reshape;reshape | solution.py:103
  62.0 2.8 %fusion.34 = bf16[2,2,49,12,32]{2,4,3,1,0:T(8,128)(2,1)} fusion(bf16[2,2,49,12,32]{2,4,3,1,0:T(8,128)(2,1)} %copy.54, f32[2,2,12,49,49]{3,4,2,1,0:T(8,128)} %get-tuple-element.16, f32[2,2,12,49]{3,2,1,0:T(8,128)S(1)} %copy-done.21), kind=kOutput, calls=%fused_computation.30 | convolution fusion | flops 7681632 | bytes 771456 | tf_op jit(solution)/shard_map/abhqk,abqhd->abkhd/dot_general | solution.py:104
  64.7 1.7 %fusion.70 = f32[2,2,12,49,49]{3,4,2,1,0:T(8,128)} fusion(bf16[2,2,49,12,32]{2,4,3,1,0:T(8,128)(2,1)S(1)} %copy-done.6, bf16[2,2,49,12,32]{2,4,3,1,0:T(8,128)(2,1)S(1)} %bitcast.92), kind=kOutput, calls=%fused_computation.130 | convolution fusion | flops 7375872 | bytes 762048 | tf_op jit(solution)/shard_map/abqhd,abkhd->abhqk/dot_general | solution.py:107
  66.4 4.0 %fusion.30 = bf16[2,2,49,12,32]{2,4,3,1,0:T(8,128)(2,1)} fusion(bf16[2,2,49,12,32]{2,4,3,1,0:T(8,128)(2,1)S(1)} %bitcast.99, f32[2,2,12,49,49]{3,4,2,1,0:T(8,128)} %fusion.70, f32[2,2,12,49,49]{3,4,2,1,0:T(8,128)} %get-tuple-element.16, f32[2,2,12,49]{3,2,1,0:T(8,128)S(1)} %copy-done.21), kind=kOutput, calls=%fused_computation.28 | convolution fusion | flops 8260272 | bytes 1232448 | tf_op jit(solution)/shard_map/abhqk,abkhd->abqhd/dot_general | solution.py:114
  70.4 4.0 %fusion.27 = bf16[2,2,49,12,32]{2,4,3,1,0:T(8,128)(2,1)} fusion(bf16[2,2,49,12,32]{2,4,3,1,0:T(8,128)(2,1)S(1)} %bitcast.101, f32[2,2,12,49,49]{3,4,2,1,0:T(8,128)} %fusion.70, f32[2,2,12,49,49]{3,4,2,1,0:T(8,128)} %get-tuple-element.16, f32[2,2,12,49]{3,2,1,0:T(8,128)S(1)} %copy-done.21), kind=kOutput, calls=%fused_computation.27 | convolution fusion | flops 8260272 | bytes 1232448 | tf_op jit(solution)/shard_map/abhqk,abqhd->abkhd/dot_general | solution.py:117
  75.2 2.4 %copy.61 = bf16[2,2,49,12,32]{4,3,1,2,0:T(8,128)(2,1)S(1)} copy(bf16[2,2,49,12,32]{2,4,3,1,0:T(8,128)(2,1)} %fusion.34) | data formatting | bytes 301056 | tf_op jit(solution)/shard_map/abhqk,abqhd->abkhd/transpose | solution.py:104
  77.6 1.4 concatenate.76
  79.0 2.4 %copy.58 = bf16[2,2,49,12,32]{4,3,1,2,0:T(8,128)(2,1)S(1)} copy(bf16[2,2,49,12,32]{2,4,3,1,0:T(8,128)(2,1)} %fusion.27) | data formatting | bytes 301056 | tf_op jit(solution)/shard_map/abhqk,abqhd->abkhd/transpose | solution.py:117
  81.4 1.4 concatenate.75
  82.7 2.4 %copy.56 = bf16[2,2,49,12,32]{4,3,1,2,0:T(8,128)(2,1)S(1)} copy(bf16[2,2,49,12,32]{2,4,3,1,0:T(8,128)(2,1)} %fusion.30) | data formatting | bytes 301056 | tf_op jit(solution)/shard_map/abhqk,abkhd->abqhd/transpose | solution.py:114
  85.1 1.4 concatenate.74
  86.5 1.5 %maximum_bitcast_fusion = bf16[2,7,2,7,1152]{4,2,3,1,0:T(2,128)(2,1)S(1)} fusion(bf16[2,2,7,7,384]{4,1,3,2,0:T(2,128)(2,1)} %concatenate.76, bf16[2,2,7,7,384]{4,1,3,2,0:T(2,128)(2,1)} %concatenate.75, bf16[2,2,7,7,384]{4,1,3,2,0:T(2,128)(2,1)} %concatenate.74), kind=kLoop, calls=%fused_computation.41 | loop fusion | flops 1354752 | bytes 903168 | tf_op jit(solution)/shard_map/transpose | solution.py:21
  89.0 2.4 %convolution_convert_fusion = bf16[384,1152]{1,0:T(8,128)(2,1)} fusion(bf16[196,384]{1,0:T(8,128)(2,1)S(1)} %copy-done.7, bf16[196,1152]{1,0:T(8,128)(2,1)} %reshape_reshape.25), kind=kOutput, calls=%fused_computation.2 | convolution fusion | flops 173850624 | bytes 1486848 | tf_op jit(solution)/shard_map/dot_general | solution.py:131
  91.4 3.0 %concatenate.83 = bf16[2,2,2,2,2,13824]{5,4,3,2,1,0:T(2,128)(2,1)} reshape(bf16[384,1152]{1,0:T(8,128)(2,1)} %convolution_convert_fusion) | data formatting | bytes 1769472 | tf_op jit(solution)/shard_map/concatenate | solution.py:152
  94.4 2.0 %copy_dynamic-update-slice_fusion = bf16[2,2,2,2,2,18432]{5,3,4,2,1,0:T(2,128)(2,1)S(1)} fusion(bf16[2,2,2,2,2,13824]{5,4,3,2,1,0:T(2,128)(2,1)} %concatenate.83), kind=kLoop, calls=%fused_computation.36 | loop fusion | bytes 1769472
  96.7 1.0 copy-done.1
  97.7 1.2 constant_dynamic-slice_fusion.4
  100.1 1.2 reshape.365
  102.3 2.0 %fusion.64 = (f32[14,14]{1,0:T(8,128)S(1)}, f32[14,14]{1,0:T(8,128)S(1)}, f32[14,14,384]{2,1,0:T(8,128)S(1)}) fusion(f32[3,14,384]{2,1,0:T(8,128)} %copy-done.9, f32[11,14,384]{2,1,0:T(8,128)S(1)} %slice.128, bf16[14,14,1152]{2,1,0:T(8,128)(2,1)} %dot_general.62, bf16[384,1152]{1,0:T(8,128)(2,1)} %param.8), kind=kOutput, calls=%fused_computation.125 | convolution fusion | flops 173708928 | bytes 1940000 | tf_op jit(solution)/shard_map/dot_general | solution.py:209
  104.3 1.7 %add_convert_fusion = bf16[2,2,2,2,1,18432]{5,3,4,2,1,0:T(2,128)(2,1)S(1)} fusion(bf16[2,2,2,2,1,18432]{5,3,4,2,1,0:T(2,128)(2,1)} %collective-permute-done.4, bf16[2,2,2,2,2,18432]{5,3,4,2,1,0:T(2,128)(2,1)S(1)} %copy-done.2, s32[]{:T(128)S(6)} %select_n.71), kind=kLoop, calls=%fused_computation.31 | loop fusion | flops 1179648 | bytes 1769476 | tf_op jit(solution)/shard_map/convert_element_type | solution.py:162
  106.6 9.1 %collective-permute-done.5 = bf16[2,2,1,2,1,18432]{5,3,4,2,1,0:T(2,128)(2,1)S(1)} collective-permute-done((bf16[2,2,1,2,1,18432]{5,3,4,2,1,0:T(2,128)(2,1)S(1)}, bf16[2,2,1,2,1,18432]{5,3,4,2,1,0:T(2,128)(2,1)S(1)}, u32[]{:S(2)}, u32[]{:S(2)}) %collective-permute-start.5) | collective-permute-done | bytes 294944 | tf_op jit(solution)/shard_map/ppermute | solution.py:160
  116.3 1.6 %collective-permute-start.6 = (bf16[2,2,1,1,1,18432]{5,3,4,2,1,0:T(2,128)(2,1)S(1)}, bf16[2,2,1,1,1,18432]{5,3,4,2,1,0:T(2,128)(2,1)S(1)}, u32[]{:S(2)}, u32[]{:S(2)}) collective-permute-start(bf16[2,2,1,1,1,18432]{5,3,4,2,1,0:T(2,128)(2,1)S(1)} %constant_dynamic-slice_fusion.2), channel_id=1, source_target_pairs={{0,2},{1,3},{2,0},{3,1},{4,6},{5,7},{6,4},{7,5},{8,10},{9,11},{10,... | collective-permute-start | bytes 442376 | tf_op jit(solution)/shard_map/ppermute | solution.py:160
  118.3 6.6 %collective-permute-done.6 = bf16[2,2,1,1,1,18432]{5,3,4,2,1,0:T(2,128)(2,1)S(1)} collective-permute-done((bf16[2,2,1,1,1,18432]{5,3,4,2,1,0:T(2,128)(2,1)S(1)}, bf16[2,2,1,1,1,18432]{5,3,4,2,1,0:T(2,128)(2,1)S(1)}, u32[]{:S(2)}, u32[]{:S(2)}) %collective-permute-start.6) | collective-permute-done | bytes 147488 | tf_op jit(solution)/shard_map/ppermute | solution.py:160
  125.7 8.0 %collective-permute-done.7 = bf16[1,2,1,1,1,18432]{5,3,4,2,1,0:T(2,128)(2,1)S(1)} collective-permute-done((bf16[1,2,1,1,1,18432]{5,3,4,2,1,0:T(2,128)(2,1)S(1)}, bf16[1,2,1,1,1,18432]{5,3,4,2,1,0:T(2,128)(2,1)S(1)}, u32[]{:S(2)}, u32[]{:S(2)}) %collective-permute-start.7) | collective-permute-done | bytes 73760 | tf_op jit(solution)/shard_map/ppermute | solution.py:160
  134.8 3.6 %collective-permute-done.8 = bf16[1,1,1,1,1,18432]{5,3,4,2,1,0:T(2,128)(2,1)S(1)} collective-permute-done((bf16[1,1,1,1,1,18432]{5,3,4,2,1,0:T(2,128)(2,1)S(1)}, bf16[1,1,1,1,1,18432]{5,3,4,2,1,0:T(2,128)(2,1)S(1)}, u32[]{:S(2)}, u32[]{:S(2)}) %collective-permute-start.8) | collective-permute-done | bytes 36896 | tf_op jit(solution)/shard_map/ppermute | solution.py:160
  (133 shorter events, 24.1 us)
Async XLA Ops:
  0.6 45.8 %copy-start = (bf16[1536,768]{1,0:T(8,128)(2,1)S(1)}, bf16[1536,768]{1,0:T(8,128)(2,1)}, u32[]{:S(2)}) copy-start(bf16[1536,768]{1,0:T(8,128)(2,1)} %param.10) | copy-start | bytes 7077892
  0.6 11.6 %copy-start.14 = (bf16[1,14,14,384]{3,2,1,0:T(8,128)(2,1)S(1)}, bf16[1,14,14,384]{3,2,1,0:T(8,128)(2,1)}, u32[]{:S(2)}) copy-start(bf16[1,14,14,384]{3,2,1,0:T(8,128)(2,1)} %param.6) | copy-start | bytes 451588
  2.3 12.0 %collective-permute-start = (bf16[14,3,384]{2,1,0:T(4,128)(2,1)}, bf16[14,3,384]{2,1,0:T(4,128)(2,1)S(1)}, u32[]{:S(2)}, u32[]{:S(2)}) collective-permute-start(bf16[14,3,384]{2,1,0:T(4,128)(2,1)} %slice.127), channel_id=1, source_target_pairs={{4,0},{8,4},{12,8},{16,12},{20,16},{24,20},{28,24},{0,28},{5,1},{9... | collective-permute-start | bytes 96776 | tf_op jit(solution)/shard_map/ppermute | solution.py:10
  14.3 3.5 %copy-start.3 = (bf16[384,1152]{1,0:T(8,128)(2,1)S(1)}, bf16[384,1152]{1,0:T(8,128)(2,1)}, u32[]{:S(2)}) copy-start(bf16[384,1152]{1,0:T(8,128)(2,1)} %param.8) | copy-start | bytes 2654212
  14.9 0.6 copy-start.9
  21.5 2.6 %copy-start.18 = (f32[49,49,12]{0,1,2:T(8,128)S(1)}, f32[49,49,12]{0,1,2:T(8,128)}, u32[]{:S(2)}) copy-start(f32[49,49,12]{0,1,2:T(8,128)} %copy.46) | copy-start | bytes 345748
  24.1 3.2 %copy-start.4 = (bf16[2,2,49,384]{2,3,1,0:T(8,128)(2,1)}, bf16[2,2,49,384]{2,3,1,0:T(8,128)(2,1)S(1)}, u32[]{:S(2)}) copy-start(bf16[2,2,49,384]{2,3,1,0:T(8,128)(2,1)S(1)} %copy.43) | copy-start | bytes 451588
  27.3 0.6 copy-start.20
  36.5 6.8 %collective-permute-start.1 = (bf16[14,3,384]{2,1,0:T(4,128)(2,1)S(1)}, bf16[14,3,384]{2,1,0:T(4,128)(2,1)S(1)}, u32[]{:S(2)}, u32[]{:S(2)}) collective-permute-start(bf16[14,3,384]{2,1,0:T(4,128)(2,1)S(1)} %slice.168), channel_id=1, source_target_pairs={{28,0},{0,4},{4,8},{8,12},{12,16},{16,20},{20,24},{24,28},{29,1},{... | collective-permute-start | bytes 96776 | tf_op jit(solution)/shard_map/ppermute | solution.py:10
  43.3 3.1 %copy-start.19 = (bf16[1,7,7,768]{3,2,1,0:T(8,128)(2,1)S(1)}, bf16[1,7,7,768]{3,2,1,0:T(8,128)(2,1)}, u32[]{:S(2)}) copy-start(bf16[1,7,7,768]{3,2,1,0:T(8,128)(2,1)} %param.11) | copy-start | bytes 225796
  50.5 0.7 copy-start.15
  50.6 4.3 %collective-permute-start.2 = (bf16[14,3,384]{2,1,0:T(4,128)(2,1)S(1)}, bf16[14,3,384]{2,1,0:T(4,128)(2,1)S(1)}, u32[]{:S(2)}, u32[]{:S(2)}) collective-permute-start(bf16[14,3,384]{2,1,0:T(4,128)(2,1)S(1)} %slice.140), channel_id=1, source_target_pairs={{4,0},{8,4},{12,8},{16,12},{20,16},{24,20},{28,24},{0,28},{5,1},{9... | collective-permute-start | bytes 96776 | tf_op jit(solution)/shard_map/ppermute | solution.py:10
  51.3 6.3 %copy-start.13 = (bf16[384,384]{1,0:T(8,128)(2,1)S(1)}, bf16[384,384]{1,0:T(8,128)(2,1)}, u32[]{:S(2)}) copy-start(bf16[384,384]{1,0:T(8,128)(2,1)} %param.9) | copy-start | bytes 884740
  57.9 4.1 %copy-start.21 = (f32[2,2,12,49]{3,2,1,0:T(8,128)S(1)}, f32[2,2,12,49]{3,2,1,0:T(8,128)}, u32[]{:S(2)}) copy-start(f32[2,2,12,49]{3,2,1,0:T(8,128)} %copy-done.20) | copy-start | bytes 28228
  62.0 2.8 %copy-start.5 = (bf16[2,2,49,384]{2,3,1,0:T(8,128)(2,1)S(1)}, bf16[2,2,49,384]{2,3,1,0:T(8,128)(2,1)}, u32[]{:S(2)}) copy-start(bf16[2,2,49,384]{2,3,1,0:T(8,128)(2,1)} %copy-done.4) | copy-start | bytes 451588
  62.0 2.8 %copy-start.6 = (bf16[2,2,49,12,32]{2,4,3,1,0:T(8,128)(2,1)S(1)}, bf16[2,2,49,12,32]{2,4,3,1,0:T(8,128)(2,1)}, u32[]{:S(2)}) copy-start(bf16[2,2,49,12,32]{2,4,3,1,0:T(8,128)(2,1)} %copy.54) | copy-start | bytes 451588
  64.7 1.7 %copy-start.16 = (bf16[2,2,49,384]{2,3,1,0:T(8,128)(2,1)S(1)}, bf16[2,2,49,384]{2,3,1,0:T(8,128)(2,1)}, u32[]{:S(2)}) copy-start(bf16[2,2,49,384]{2,3,1,0:T(8,128)(2,1)} %copy.45) | copy-start | bytes 451588
  66.4 4.0 %copy-start.17 = (bf16[2,2,49,384]{2,3,1,0:T(8,128)(2,1)S(1)}, bf16[2,2,49,384]{2,3,1,0:T(8,128)(2,1)}, u32[]{:S(2)}) copy-start(bf16[2,2,49,384]{2,3,1,0:T(8,128)(2,1)} %copy.44) | copy-start | bytes 451588
  70.4 4.0 %copy-start.12 = (bf16[384,384]{1,0:T(8,128)(2,1)S(1)}, bf16[384,384]{1,0:T(8,128)(2,1)}, u32[]{:S(2)}) copy-start(bf16[384,384]{1,0:T(8,128)(2,1)} %convolution_convert_fusion.4) | copy-start | bytes 884740
  86.5 2.5 %copy-start.7 = (bf16[196,384]{1,0:T(8,128)(2,1)S(1)}, bf16[196,384]{1,0:T(8,128)(2,1)}, u32[]{:S(2)}) copy-start(bf16[196,384]{1,0:T(8,128)(2,1)} %convert_element_type.200) | copy-start | bytes 451588
  91.4 5.0 %copy-start.11 = (bf16[2,2,2,2,2,4608]{5,4,3,2,1,0:T(2,128)(2,1)S(1)}, bf16[2,2,2,2,2,4608]{5,4,3,2,1,0:T(2,128)(2,1)}, u32[]{:S(2)}) copy-start(bf16[2,2,2,2,2,4608]{5,4,3,2,1,0:T(2,128)(2,1)} %concatenate.84) | copy-start | bytes 884740
  94.4 4.5 %copy-start.8 = (f32[49,1536]{1,0:T(8,128)S(1)}, f32[49,1536]{1,0:T(8,128)}, u32[]{:S(2)}) copy-start(f32[49,1536]{1,0:T(8,128)} %reshape.363) | copy-start | bytes 903172
  96.7 1.0 copy-start.1
  98.9 5.4 %collective-permute-start.4 = (bf16[2,2,2,2,1,18432]{5,3,4,2,1,0:T(2,128)(2,1)}, bf16[2,2,2,2,1,18432]{5,3,4,2,1,0:T(2,128)(2,1)}, u32[]{:S(2)}, u32[]{:S(2)}) collective-permute-start(bf16[2,2,2,2,1,18432]{5,3,4,2,1,0:T(2,128)(2,1)} %constant_dynamic-slice_fusion.4), channel_id=1, source_target_pairs={{0,1},{1,0},{2,3},{3,2},{4,5},{5,4},{6,7},{7,6},{8,9},{9,8},{10,11... | collective-permute-start | bytes 1769480 | tf_op jit(solution)/shard_map/ppermute | solution.py:160
  102.2 2.0 %copy-start.2 = (bf16[2,2,2,2,2,18432]{5,3,4,2,1,0:T(2,128)(2,1)S(1)}, bf16[2,2,2,2,2,18432]{5,3,4,2,1,0:T(2,128)(2,1)}, u32[]{:S(2)}) copy-start(bf16[2,2,2,2,2,18432]{5,3,4,2,1,0:T(2,128)(2,1)} %copy-done.1) | copy-start | bytes 3538948
  104.3 2.1 %copy-start.10 = (f32[3,14,384]{2,1,0:T(8,128)S(1)}, f32[3,14,384]{2,1,0:T(8,128)}, u32[]{:S(2)}) copy-start(f32[3,14,384]{2,1,0:T(8,128)} %copy-done.9) | copy-start | bytes 193540
  106.2 9.5 %collective-permute-start.5 = (bf16[2,2,1,2,1,18432]{5,3,4,2,1,0:T(2,128)(2,1)S(1)}, bf16[2,2,1,2,1,18432]{5,3,4,2,1,0:T(2,128)(2,1)S(1)}, u32[]{:S(2)}, u32[]{:S(2)}) collective-permute-start(bf16[2,2,1,2,1,18432]{5,3,4,2,1,0:T(2,128)(2,1)S(1)} %constant_dynamic-slice_fusion.3), channel_id=1, source_target_pairs={{0,4},{4,0},{8,12},{12,8},{16,20},{20,16},{24,28},{28,24},{1,5},{5... | collective-permute-start | bytes 884744 | tf_op jit(solution)/shard_map/ppermute | solution.py:160
  116.3 8.6 %collective-permute-start.6 = (bf16[2,2,1,1,1,18432]{5,3,4,2,1,0:T(2,128)(2,1)S(1)}, bf16[2,2,1,1,1,18432]{5,3,4,2,1,0:T(2,128)(2,1)S(1)}, u32[]{:S(2)}, u32[]{:S(2)}) collective-permute-start(bf16[2,2,1,1,1,18432]{5,3,4,2,1,0:T(2,128)(2,1)S(1)} %constant_dynamic-slice_fusion.2), channel_id=1, source_target_pairs={{0,2},{1,3},{2,0},{3,1},{4,6},{5,7},{6,4},{7,5},{8,10},{9,11},{10,... | collective-permute-start | bytes 442376 | tf_op jit(solution)/shard_map/ppermute | solution.py:160
  118.0 7.7 %collective-permute-start.3 = (bf16[14,3,384]{2,1,0:T(4,128)(2,1)S(1)}, bf16[14,3,384]{2,1,0:T(4,128)(2,1)S(1)}, u32[]{:S(2)}, u32[]{:S(2)}) collective-permute-start(bf16[14,3,384]{2,1,0:T(4,128)(2,1)S(1)} %fusion.54), channel_id=1, source_target_pairs={{28,0},{0,4},{4,8},{8,12},{12,16},{16,20},{20,24},{24,28},{29,1},{... | collective-permute-start | bytes 96776 | tf_op jit(solution)/shard_map/ppermute | solution.py:10
  125.6 8.1 %collective-permute-start.7 = (bf16[1,2,1,1,1,18432]{5,3,4,2,1,0:T(2,128)(2,1)S(1)}, bf16[1,2,1,1,1,18432]{5,3,4,2,1,0:T(2,128)(2,1)S(1)}, u32[]{:S(2)}, u32[]{:S(2)}) collective-permute-start(bf16[1,2,1,1,1,18432]{5,3,4,2,1,0:T(2,128)(2,1)S(1)} %constant_dynamic-slice_fusion.1), channel_id=1, source_target_pairs={{0,16},{4,20},{8,24},{12,28},{16,0},{20,4},{24,8},{28,12},{1,17},{... | collective-permute-start | bytes 221192 | tf_op jit(solution)/shard_map/ppermute | solution.py:160
  134.0 4.4 %collective-permute-start.8 = (bf16[1,1,1,1,1,18432]{5,3,4,2,1,0:T(2,128)(2,1)S(1)}, bf16[1,1,1,1,1,18432]{5,3,4,2,1,0:T(2,128)(2,1)S(1)}, u32[]{:S(2)}, u32[]{:S(2)}) collective-permute-start(bf16[1,1,1,1,1,18432]{5,3,4,2,1,0:T(2,128)(2,1)S(1)} %constant_dynamic-slice_fusion), channel_id=1, source_target_pairs={{0,8},{4,12},{8,0},{12,4},{16,24},{20,28},{24,16},{28,20},{1,9},{5... | collective-permute-start | bytes 110600 | tf_op jit(solution)/shard_map/ppermute | solution.py:160

commit v2 on v1

v2 whole, which is shorter than its diff:
```python
import functools

import jax
import jax.numpy as jnp
import numpy as np
from jax import lax
from jax.experimental import pallas as pl
from jax.experimental.pallas import tpu as pltpu
from jax.sharding import PartitionSpec as P

WINDOW = 7
SHIFT = 3
SLOT = 64
LANES = 128
EPS = 1e-05


def up(value, step):
    return -(-value // step) * step


def dot(left, right):
    return lax.dot_general(left, right, (((1,), (0,)), ((), ())), preferred_element_type=jnp.float32)


def dot_t(left, right):
    return lax.dot_general(left, right, (((1,), (1,)), ((), ())), preferred_element_type=jnp.float32)


def pick(select, values):
    return dot(select, values).astype(jnp.bfloat16)


class Grid:
    def __init__(self, rows, cols, heads, channels):
        self.rows, self.cols, self.heads, self.channels = rows, cols, heads, channels
        self.bands = rows // WINDOW
        self.own_across = cols // WINDOW
        self.east, self.west = 2 * WINDOW - SHIFT - 1, WINDOW - SHIFT
        own = [(a, w) for a in range(self.bands) for w in range(1, self.own_across + 1)]
        halo = [(a, w) for w in (0, self.own_across + 1) for a in range(self.bands)]
        self.windows = own + halo
        self.own_windows = len(own)
        self.stride = up(cols, 16)
        self.own_rows = rows * self.stride
        self.east_rows = up(rows * self.east, 16)
        self.west_rows = up(rows * self.west, 16)
        self.token_rows = self.own_rows + self.east_rows + self.west_rows
        self.quad_rows, self.quad_cols = rows // 2, cols // 2
        self.quad_stride = up(self.quad_cols + 1, 8)
        self.quad_count = up(self.quad_rows * (self.quad_stride + 1), 16)
        self.cot_stride = up(self.quad_cols, 16)
        self.cot_own = self.quad_rows * self.cot_stride
        self.cot_halo = up(2 * self.quad_rows, 16)
        self.back_rows = up(rows * SHIFT, 16)

    def source(self, row, col):
        if col < 0:
            return self.own_rows + self.east_rows + row * self.west + col + self.west
        if col < self.cols:
            return row * self.stride + col
        return self.own_rows + row * self.east + col - self.cols

    def window_row(self, row, col):
        line = (row - SHIFT) % self.rows
        across, place = divmod(col + self.west, WINDOW)
        window = self.windows.index((line // WINDOW, across))
        return window * SLOT + (line % WINDOW) * WINDOW + place

    def quad_row(self, row, col):
        i, j = row // 2, col // 2
        phase = 2 * (col % 2) + row % 2
        at = i * self.quad_stride + j if j < self.quad_stride else self.quad_rows * self.quad_stride + i
        return phase * self.quad_count + at

    def onehot(self, shape, pairs):
        out = np.zeros(shape, np.float32)
        for i, j in pairs:
            out[i, j] = 1
        return jnp.asarray(out, jnp.bfloat16)

    def cells(self, first, last):
        return [(r, c) for r in range(self.rows) for c in range(first, last)]

    def to_windows(self):
        cells = self.cells(-self.west, self.cols + self.east)
        pairs = [(self.window_row(r, c), self.source(r, c)) for r, c in cells]
        return self.onehot((len(self.windows) * SLOT, self.token_rows), pairs)

    def to_quads(self):
        cells = self.cells(0, self.cols + 4)
        pairs = [(self.quad_row(r, c), self.window_row(r, c)) for r, c in cells]
        return self.onehot((4 * self.quad_count, len(self.windows) * SLOT), pairs)

    def from_quads(self):
        cells = self.cells(SHIFT, self.cols + SHIFT)
        pairs = [(self.window_row(r, c), self.quad_row(r, c)) for r, c in cells]
        return self.onehot((self.own_windows * SLOT, 4 * self.quad_count), pairs)

    def quads_to_grid(self):
        pairs = [(self.source(r, c), self.quad_row(r, c)) for r, c in self.cells(0, self.cols)]
        return self.onehot((self.own_rows, 4 * self.quad_count), pairs)

    def windows_to_grid(self):
        pairs = [(self.source(r, c), self.window_row(r, c)) for r, c in self.cells(SHIFT, self.cols)]
        return self.onehot((self.own_rows, self.own_windows * SLOT), pairs)

    def windows_to_back(self):
        cells = self.cells(self.cols, self.cols + SHIFT)
        pairs = [(r * SHIFT + c - self.cols, self.window_row(r, c)) for r, c in cells]
        return self.onehot((self.back_rows, self.own_windows * SLOT), pairs)

    def back_to_grid(self):
        pairs = [(self.source(r, c), r * SHIFT + c) for r, c in self.cells(0, SHIFT)]
        return self.onehot((self.own_rows, self.back_rows), pairs)

    def pack_east(self):
        pairs = [(r * self.east + c, self.source(r, c)) for r, c in self.cells(0, self.east)]
        return self.onehot((self.east_rows, self.own_rows), pairs)

    def pack_west(self):
        first = self.cols - self.west
        pairs = [(r * self.west + c - first, self.source(r, c)) for r, c in self.cells(first, self.cols)]
        return self.onehot((self.west_rows, self.own_rows), pairs)

    def pack_cot(self):
        pairs = [(2 * i + j, i * self.cot_stride + j) for i in range(self.quad_rows) for j in range(2)]
        return self.onehot((self.cot_halo, self.cot_own), pairs)

    def cot_to_quads(self):
        pairs = []
        for i in range(self.quad_rows):
            for j in range(self.quad_cols + 2):
                own = i * self.cot_stride + j
                source = own if j < self.quad_cols else self.cot_own + 2 * i + j - self.quad_cols
                pairs.append((self.quad_row(2 * i, 2 * j), source))
        return self.onehot((self.quad_count, self.cot_own + self.cot_halo), pairs)


def normalize(values):
    centred = values - jnp.mean(values, -1, keepdims=True)
    inverse_std = lax.rsqrt(jnp.mean(centred * centred, -1, keepdims=True) + EPS)
    return centred * inverse_std, inverse_std


def spread(ref, grid_ref, stride):
    ref[0 : grid_ref.shape[0] * stride, :] = jnp.zeros((grid_ref.shape[0] * stride, ref.shape[1]), ref.dtype)
    for line in range(grid_ref.shape[0]):
        ref[line * stride : line * stride + grid_ref.shape[1], :] = grid_ref[line]


def pre_kernel(grid, x, cot, pack_east, pack_west, pack_cot, to_prev, to_next, tokens, quads):
    spread(tokens, x, grid.stride)
    spread(quads, cot, grid.cot_stride)
    channels = grid.channels
    to_prev[0 : grid.east_rows, :] = pick(pack_east[...], tokens[...])
    halo = pick(pack_cot[...], quads[...])
    for part in range(halo.shape[1] // channels):
        first = grid.east_rows + part * grid.cot_halo
        to_prev[first : first + grid.cot_halo, :] = halo[:, part * channels : (part + 1) * channels]
    to_next[...] = pick(pack_west[...], tokens[...])


def head_sum(stacked, head_mask, per_group):
    total = None
    for head in range(per_group):
        part = stacked[head * SLOT : (head + 1) * SLOT, :]
        part = jnp.where(head_mask[head * SLOT : (head + 1) * SLOT, :] > 0, part, 0.0)
        total = part if total is None else total + part
    return total


def main_kernel(
    grid, x, from_east, from_west, cot, attend_weight, output_weight, merge_weight, bias, mask, head_mask,
    to_windows, to_quads, from_quads, cot_to_quads, row_order,
    kept, sent, projected_grad, normed_out, std_out, hidden_grad_out, quad16_out,
    tokens, quads, projected, attended, probs, outer,
):
    channels, heads = grid.channels, grid.heads
    head_size = channels // heads
    scale = head_size ** (-0.5)
    per_group = LANES // head_size
    groups = heads // per_group
    own = grid.own_windows * SLOT
    total_windows = len(grid.windows)

    spread(tokens, x, grid.stride)
    tokens[grid.own_rows : grid.own_rows + grid.east_rows, :] = from_east[0 : grid.east_rows, :]
    tokens[grid.own_rows + grid.east_rows :, :] = from_west[...]
    spread(quads, cot, grid.cot_stride)
    for part in range(cot.shape[2] // channels):
        first = grid.east_rows + part * grid.cot_halo
        quads[grid.cot_own :, part * channels : (part + 1) * channels] = from_east[first : first + grid.cot_halo, :]

    windowed = dot(to_windows[...], tokens[...])
    normed, inverse_std = normalize(windowed)
    rolled = normed.astype(jnp.bfloat16)
    normed_out[...] = normed[:own]
    std_out[...] = inverse_std[:own]
    projected[...] = dot(rolled, attend_weight[...]).astype(jnp.bfloat16)

    mask_all = head_mask[...]

    def forward(window, carry):
        rows = pl.ds(pl.multiple_of(window * SLOT, SLOT), SLOT)
        band = jnp.where(
            window < grid.own_windows, window // grid.own_across, (window - grid.own_windows) % grid.bands
        )
        extra = mask[band]
        for group in range(groups):
            lanes = group * LANES
            query = projected[rows, lanes : lanes + LANES]
            key = projected[rows, channels + lanes : channels + lanes + LANES]
            value = projected[rows, 2 * channels + lanes : 2 * channels + lanes + LANES]
            spread_query = jnp.concatenate([query] * per_group, 0) * mask_all
            scores = dot_t(key, spread_query) * scale + bias[group] + extra
            weights = jnp.exp(scores - jnp.max(scores, 0, keepdims=True))
            prob = weights / jnp.sum(weights, 0, keepdims=True)

            @pl.when(window < grid.own_windows)
            def _():
                probs[jnp.minimum(window, grid.own_windows - 1) * groups + group] = prob

            mixed = dot(prob.astype(jnp.bfloat16).T, value)
            attended[rows, lanes : lanes + LANES] = head_sum(mixed, mask_all, per_group).astype(jnp.bfloat16)
        return carry

    lax.fori_loop(0, total_windows, forward, 0)

    attended_quads = pick(to_quads[...], attended[...])
    feature_quads = dot(to_quads[...], windowed.astype(jnp.bfloat16))
    branch = dot(attended_quads, output_weight[...])
    hidden = (feature_quads + branch).astype(jnp.bfloat16).astype(jnp.float32)
    count = grid.quad_count
    phases = [hidden[k * count : (k + 1) * count] for k in range(4)]
    width = 4 * channels
    mean = sum(jnp.sum(phase, -1, keepdims=True) for phase in phases) / width
    centred = [phase - mean for phase in phases]
    variance = sum(jnp.sum(phase * phase, -1, keepdims=True) for phase in centred) / width
    quad_std = lax.rsqrt(variance + EPS)
    quad_normed = [phase * quad_std for phase in centred]
    cot_quads = pick(cot_to_quads[...], quads[...])
    quad_grads = []
    for k in range(4):
        quad16_out[k * count : (k + 1) * count, :] = quad_normed[k].astype(jnp.bfloat16)
        quad_grads.append(dot_t(cot_quads, merge_weight[k * channels : (k + 1) * channels, :]))
    first = sum(jnp.sum(part, -1, keepdims=True) for part in quad_grads) / width
    second = sum(jnp.sum(part * n, -1, keepdims=True) for part, n in zip(quad_grads, quad_normed)) / width
    for k in range(4):
        hidden_grad_out[k * count : (k + 1) * count, :] = (
            quad_std * (quad_grads[k] - first - quad_normed[k] * second)
        ).astype(jnp.bfloat16)

    branch_grad = pick(from_quads[...], hidden_grad_out[...])
    outer[...] = dot_t(branch_grad, output_weight[...]).astype(jnp.bfloat16)

    def backward(window, carry):
        rows = pl.ds(pl.multiple_of(window * SLOT, SLOT), SLOT)
        for group in range(groups):
            lanes = group * LANES
            query = projected[rows, lanes : lanes + LANES]
            key = projected[rows, channels + lanes : channels + lanes + LANES]
            value = projected[rows, 2 * channels + lanes : 2 * channels + lanes + LANES]
            grads = outer[rows, lanes : lanes + LANES]
            spread_query = jnp.concatenate([query] * per_group, 0) * mask_all
            spread_grads = jnp.concatenate([grads] * per_group, 0) * mask_all
            prob = probs[window * groups + group]
            value_grad = dot(prob.astype(jnp.bfloat16), spread_grads)
            score_grad = dot_t(value, spread_grads)
            inner = jnp.sum(prob * score_grad, 0, keepdims=True)
            soft = (prob * (score_grad - inner) * scale).astype(jnp.bfloat16)
            key_grad = dot(soft, spread_query)
            query_grad = head_sum(dot(soft.T, key), mask_all, per_group)
            projected_grad[rows, lanes : lanes + LANES] = query_grad.astype(jnp.bfloat16)
            projected_grad[rows, channels + lanes : channels + lanes + LANES] = key_grad.astype(jnp.bfloat16)
            projected_grad[rows, 2 * channels + lanes : 2 * channels + lanes + LANES] = value_grad.astype(
                jnp.bfloat16
            )
        return carry

    lax.fori_loop(0, grid.own_windows, backward, 0)

    columns = lax.broadcasted_iota(jnp.int32, (channels, channels), 1)
    order = jnp.where(columns == row_order[...], 1.0, 0.0).astype(jnp.bfloat16)
    rolled_t = dot_t(order, rolled[:own]).astype(jnp.bfloat16)
    attended_t = dot_t(order, attended[0:own, :]).astype(jnp.bfloat16)
    attend_part = dot(rolled_t, projected_grad[...]).astype(jnp.bfloat16)
    output_part = dot(attended_t, branch_grad).astype(jnp.bfloat16)
    half = channels // 2
    kept[:, 0 : 3 * channels] = attend_part[:half]
    sent[:, 0 : 3 * channels] = attend_part[half:]
    kept[:, 3 * channels :] = output_part[:half]
    sent[:, 3 * channels :] = output_part[half:]


def tail_kernel(
    grid, projected_grad, attend_weight, normed, inverse_std, hidden_grad, quad16, merge_weight,
    quads_to_grid, windows_to_grid, windows_to_back, part, back, merged,
):
    channels = grid.channels
    grads = dot_t(projected_grad[...], attend_weight[...])
    n = normed[...]
    first = jnp.mean(grads, -1, keepdims=True)
    second = jnp.mean(grads * n, -1, keepdims=True)
    rolled_grad = inverse_std[...] * (grads - first - n * second)
    high = rolled_grad.astype(jnp.bfloat16)
    low = (rolled_grad - high.astype(jnp.float32)).astype(jnp.bfloat16)
    back[...] = pick(windows_to_back[...], high)
    part[...] = (
        dot(quads_to_grid[...], hidden_grad[...])
        + dot(windows_to_grid[...], high)
        + dot(windows_to_grid[...], low)
    )
    count = grid.quad_count
    total = None
    for k in range(4):
        term = dot(quad16[k * count : (k + 1) * count, :], merge_weight[k * channels : (k + 1) * channels, :])
        total = term if total is None else total + term
    for i in range(grid.quad_rows):
        first_row = i * grid.quad_stride
        merged[i] = total[first_row : first_row + grid.quad_cols].astype(jnp.bfloat16)


def last_kernel(grid, part, back, back_to_grid, out):
    total = part[...] + dot(back_to_grid[...], back[...])
    for line in range(grid.rows):
        out[line] = total[line * grid.stride : line * grid.stride + grid.cols].astype(jnp.bfloat16)


def call(kernel, outs, *args, scratch=()):
    whole = pl.BlockSpec(memory_space=pltpu.VMEM)
    return pl.pallas_call(
        kernel,
        out_shape=outs,
        in_specs=[whole] * len(args),
        out_specs=jax.tree.map(lambda _: whole, outs),
        scratch_shapes=scratch,
        compiler_params=pltpu.CompilerParams(vmem_limit_bytes=56 * 2**20),
    )(*args)


def f32(*shape):
    return jax.ShapeDtypeStruct(shape, jnp.float32)


def b16(*shape):
    return jax.ShapeDtypeStruct(shape, jnp.bfloat16)


def window_bias(position_bias, grid):
    tokens = WINDOW * WINDOW
    place = np.arange(SLOT)
    row, col = place // WINDOW, place % WINDOW
    span = 2 * WINDOW - 1
    index = (row[None, :] - row[:, None] + WINDOW - 1) * span + (col[None, :] - col[:, None] + WINDOW - 1)
    real = (place[:, None] < tokens) & (place[None, :] < tokens)
    index = np.where(real, index, 0)
    one_hot = jnp.asarray(index.reshape(-1)[:, None] == np.arange(span * span)[None, :]).astype(jnp.float32)
    heads = grid.heads
    values = jnp.dot(one_hot, position_bias, precision=lax.Precision.HIGHEST)
    per_group = LANES // (grid.channels // heads)
    values = values.reshape(SLOT, SLOT, heads // per_group, per_group).transpose(2, 0, 3, 1)
    values = values.reshape(heads // per_group, SLOT, per_group * SLOT)
    padded = jnp.asarray(np.where(place < tokens, 0.0, -1e30), jnp.float32)
    values = values + padded[None, :, None]
    line = np.arange(grid.bands)[:, None] * WINDOW + row[None, :]
    region = (line >= grid.rows - WINDOW).astype(int) + (line >= grid.rows - SHIFT).astype(int)
    blocked = np.where(region[:, :, None] == region[:, None, :], 0.0, -100.0)
    blocked = np.where(real[None], blocked, 0.0)
    mask = jnp.asarray(np.concatenate([blocked] * per_group, 2), jnp.float32)
    return values, mask


def halving_bits():
    frame_bits = lax.axis_size("frame").bit_length() - 1
    azim_bits = lax.axis_size("azim").bit_length() - 1
    frame = [("frame", bit, 1 << bit) for bit in range(frame_bits)]
    azim = [("azim", bit, 1 << (bit + frame_bits)) for bit in range(azim_bits)]
    return frame[:1] + azim[:1] + frame[1:] + azim[1:][::-1]


def row_order(channels):
    bits = halving_bits()
    members = 1 << len(bits)
    row = np.arange(channels)
    if channels % members:
        return jnp.asarray(row, jnp.int32)[:, None]
    each = channels // members
    piece = jnp.zeros(channels, jnp.int32)
    for stage, (axis, bit, weight) in enumerate(bits):
        far = (row // each >> (len(bits) - 1 - stage)) & 1
        own = (lax.axis_index(axis) >> bit) & 1
        piece = piece + (own ^ jnp.asarray(far, jnp.int32)) * weight
    return (piece * each + jnp.asarray(row % each, jnp.int32))[:, None]


def scatter_flat(terms):
    bits = halving_bits()
    members = 1 << len(bits)
    widths = [term.size // members for term in terms]
    held = jnp.concatenate([term.reshape(members, -1) for term in terms], 1)
    held = held.reshape((2,) * len(bits) + (-1,))
    for axis, bit, weight in bits:
        dim = len(bits) - weight.bit_length()
        own = (lax.axis_index(axis) >> bit) & 1
        kept = lax.dynamic_slice_in_dim(held, own, 1, dim)
        sent = lax.dynamic_slice_in_dim(held, 1 - own, 1, dim)
        got = lax.ppermute(sent, axis, [(i, i ^ (1 << bit)) for i in range(lax.axis_size(axis))])
        total = kept.astype(jnp.float32) + got.astype(jnp.float32)
        held = total.astype(jnp.bfloat16)
    total = total.reshape(-1)
    return total[: widths[0]], total[widths[0] :]


def scatter_sum(kept, sent, channels):
    if channels % (1 << len(halving_bits())):
        whole = jnp.concatenate([kept, sent], 0)
        return scatter_flat((whole[:, : 3 * channels], whole[:, 3 * channels :]))
    for axis, bit, _ in halving_bits():
        route = [(i, i ^ (1 << bit)) for i in range(lax.axis_size(axis))]
        got = lax.ppermute(sent, axis, route)
        total = kept.astype(jnp.float32) + got.astype(jnp.float32)
        half = total.shape[0] // 2
        held = total.astype(jnp.bfloat16)
        kept, sent = held[:half], held[half:]
    return total[:, : 3 * channels].reshape(-1), total[:, 3 * channels :].reshape(-1)


def from_behind(block, axis, distance):
    size = lax.axis_size(axis)
    return lax.ppermute(block, axis, [((i - distance) % size, i) for i in range(size)])


def per_device(features, position_bias, attend_weight, output_weight, merge_weight, cotangent):
    x, cot = features[0], cotangent[0]
    rows, cols, channels = x.shape
    heads = position_bias.shape[1]
    grid = Grid(rows, cols, heads, channels)
    width = cot.shape[2]
    bf16 = jnp.bfloat16
    halo_rows = grid.east_rows + width // channels * grid.cot_halo
    to_prev, to_next = call(
        functools.partial(pre_kernel, grid),
        (b16(halo_rows, channels), b16(grid.west_rows, channels)),
        x, cot, grid.pack_east(), grid.pack_west(), grid.pack_cot(),
        scratch=[pltpu.VMEM((grid.own_rows, channels), bf16), pltpu.VMEM((grid.cot_own, width), bf16)],
    )
    from_east = from_behind(to_prev, "azim", -1)
    from_west = from_behind(to_next, "azim", 1)
    bias, mask = window_bias(position_bias, grid)
    per_group = LANES * heads // channels
    lane_head = np.arange(LANES) // (channels // heads)
    head_mask = jnp.asarray(np.repeat(np.arange(per_group), SLOT)[:, None] == lane_head[None, :]).astype(bf16)
    own = grid.own_windows * SLOT
    everything = len(grid.windows) * SLOT
    quad_rows = 4 * grid.quad_count
    half = channels // 2
    kept, sent, projected_grad, normed, inverse_std, hidden_grad, quad16 = call(
        functools.partial(main_kernel, grid),
        (
            b16(half, 4 * channels), b16(half, 4 * channels), b16(own, 3 * channels), f32(own, channels),
            f32(own, 1), b16(quad_rows, channels), b16(quad_rows, channels),
        ),
        x, from_east, from_west, cot, attend_weight, output_weight, merge_weight, bias, mask, head_mask,
        grid.to_windows(), grid.to_quads(), grid.from_quads(), grid.cot_to_quads(), row_order(channels),
        scratch=[
            pltpu.VMEM((grid.token_rows, channels), bf16),
            pltpu.VMEM((grid.cot_own + grid.cot_halo, width), bf16),
            pltpu.VMEM((everything, 3 * channels), bf16),
            pltpu.VMEM((everything, channels), bf16),
            pltpu.VMEM((grid.own_windows * heads // per_group, SLOT, per_group * SLOT), jnp.float32),
            pltpu.VMEM((own, channels), bf16),
        ],
    )
    part, back, merged = call(
        functools.partial(tail_kernel, grid),
        (f32(grid.own_rows, channels), b16(grid.back_rows, channels), b16(grid.quad_rows, grid.quad_cols, width)),
        projected_grad, attend_weight, normed, inverse_std, hidden_grad, quad16, merge_weight,
        grid.quads_to_grid(), grid.windows_to_grid(), grid.windows_to_back(),
    )
    came_back = from_behind(back, "azim", 1)
    feature_grad = call(
        functools.partial(last_kernel, grid), b16(rows, cols, channels), part, came_back, grid.back_to_grid()
    )
    attend_grad, output_grad = scatter_sum(kept, sent, channels)
    return (merged[None], feature_grad[None], attend_grad, output_grad)


def solution(mesh):
    in_specs = (P("frame", None, "azim", None), P(), P(), P(), P(), P("frame", None, "azim", None))
    out_specs = (
        P("frame", None, "azim", None),
        P("frame", None, "azim", None),
        P(("azim", "frame")),
        P(("azim", "frame")),
    )
    return jax.shard_map(
        per_device, mesh=mesh, in_specs=in_specs, out_specs=out_specs, check_vma=False
    )
```

time: 141 us -> 68.6 us (0.49)
  local copies, waits for them, and re-layouts: 52.1 us -> 4.72 us
  matrix products: 30.6 us -> 2.96 us
  Pallas kernels: 0 us -> 27.1 us
  waiting for transfers between devices: 35.6 us -> 19.2 us
  other arithmetic: 11.8 us -> 2.13 us
  starting transfers between devices: 8.56 us -> 11.4 us
    pallas_call x0 -> x4, Pallas kernels: none -> 27.1 us  [call(): pl.pallas_call(kernel, out_shape=outs, in_specs=[whole] * len(args), out_...]
    dot_general x14 -> x1, matrix products: 27.4 us -> 2.96 us  [window_bias(): values = jnp.dot(one_hot, position_bias, precision=lax.Precision.HIGHEST)]
    ppermute x5, waiting for transfers between devices: 27.3 us -> 14.7 us  [scatter_sum(): got = lax.ppermute(sent, axis, route)]
    transpose x7 -> x0, local copies, waits for them, and re-layouts: 9.28 us -> none  [the longest x1 2.38 us: attention_backward(): jnp.einsum('abhqk,abqhd->abkhd', probs16, outer, preferred_element_type=j...]
    concatenate x8 -> x0, local copies, waits for them, and re-layouts: 9.04 us -> none  [the longest x3 4.09 us: attention_backward(): jnp.concatenate([query_grad.reshape(flat_shape), key_grad.reshape(flat_sh...]
    convert_element_type x8 -> x0, local copies, waits for them, and re-layouts: 8.67 us -> none  [the longest x1 2.38 us: attention_forward(): attended.astype(jnp.bfloat16).reshape(head_shape[:3] + (channels,))]
    slice x21 -> x6, local copies, waits for them, and re-layouts: 7.77 us -> 0.07 us  [the longest x4 0.05 us: scatter_sum(): kept, sent = (held[:half], held[half:])]
    another operation x8 -> x0, local copies, waits for them, and re-layouts: 7.47 us -> none  [the longest x2 3.2 us: attention_backward(): outer = to_windows(attended_grad).reshape(queries.shape)]
  transfers between devices with their start and end apart: 9 -> 8, of which waited for: 6 -> 4; matrix products, arithmetic and copies ran while one was open for 11% -> 8% of each run, Pallas kernels for 0% -> 9%
where the time goes in v2:
time: 68.6 us; the launch traced here: 68.3 us
  Pallas kernels  27.1 us (40%)
  waiting for transfers between devices  19.2 us (28%)
  starting transfers between devices  11.4 us (17%)
  local copies, waits for them, and re-layouts  4.72 us (7%)
  matrix products  2.96 us (4%)
  other arithmetic  2.13 us (3%)
  between operations  0.83 us (1%)
    pallas_call x4, Pallas kernels, call(): pl.pallas_call(kernel, out_shape=outs, in_specs=[whole] * len(args), out_...  27.1 us
    ppermute x5, waiting for transfers between devices, scatter_sum(): got = lax.ppermute(sent, axis, route)  14.7 us
    ppermute x3, starting transfers between devices, from_behind(): lax.ppermute(block, axis, [((i - distance) % size, i) for i in range(size)])  6.6 us
    ppermute x5, starting transfers between devices, scatter_sum(): got = lax.ppermute(sent, axis, route)  4.82 us
    ppermute x3, waiting for transfers between devices, from_behind(): lax.ppermute(block, axis, [((i - distance) % size, i) for i in range(size)])  4.47 us
    dot_general x1, matrix products, window_bias(): values = jnp.dot(one_hot, position_bias, precision=lax.Precision.HIGHEST)  2.96 us
    unnamed x22, local copies, waits for them, and re-layouts  1.94 us
  transfers between devices with their start and end apart: 8, of which 4 were waited for; matrix products, arithmetic and copies ran while one was open for 8% of the time, Pallas kernels for 9%

profile of v2, /device:TPU:0, one launch (start us, length us, event | category | flops | bytes accessed | tf_op | source)
XLA Modules:
  0.0 68.3 jit_solution(17379278938904378138)
XLA Ops:
  0.6 0.0 copy-start
  0.6 1.9 %shard_map.282 = (bf16[176,384]{1,0:T(8,128)(2,1)}, bf16[64,384]{1,0:T(8,128)(2,1)}) custom-call(bf16[14,14,384]{2,1,0:T(8,128)(2,1)} %bitcast.12, bf16[7,7,768]{2,1,0:T(8,128)(2,1)} %bitcast.14, bf16[144,224]{1,0:T(8,128)(2,1)} %constant.66.clone.pack_east, bf16[64,224]{1,0:T(8,128)(2,1)} %constant.67.clone.pack_west, bf16[16,112]{1,0:T(8,128)(2,1)} %constant.68.clone.pack_cot), custom_call_target="tpu_custom_call" | custom-call | tf_op jit(solution)/shard_map/pallas_call | solution.py:332
  2.6 3.0 %collective-permute-start.1 = (bf16[64,384]{1,0:T(8,128)(2,1)}, bf16[64,384]{1,0:T(8,128)(2,1)S(1)}, u32[]{:S(2)}, u32[]{:S(2)}) collective-permute-start(bf16[64,384]{1,0:T(8,128)(2,1)} %get-tuple-element.17), channel_id=1, source_target_pairs={{28,0},{0,4},{4,8},{8,12},{12,16},{16,20},{20,24},{24,28},{29,1},{... | collective-permute-start | bytes 147464 | tf_op jit(solution)/shard_map/ppermute | solution.py:431
  5.6 3.0 %collective-permute-start = (bf16[176,384]{1,0:T(8,128)(2,1)}, bf16[176,384]{1,0:T(8,128)(2,1)S(1)}, u32[]{:S(2)}, u32[]{:S(2)}) collective-permute-start(bf16[176,384]{1,0:T(8,128)(2,1)} %get-tuple-element.16), channel_id=1, source_target_pairs={{4,0},{8,4},{12,8},{16,12},{20,16},{24,20},{28,24},{0,28},{5,1},{9... | collective-permute-start | bytes 405512 | tf_op jit(solution)/shard_map/ppermute | solution.py:431
  8.6 0.0 copy-done
  8.6 3.0 %fusion = f32[4096,12]{0,1:T(8,128)S(1)} fusion(pred[4096,169]{1,0:T(32,128)(4,1)} %constant.69.clone, f32[169,12]{0,1:T(8,128)S(1)} %copy-done), kind=kOutput, calls=%fused_computation.8 | convolution fusion | flops 99680256 | bytes 896944 | tf_op jit(solution)/shard_map/dot_general | solution.py:360
  11.6 0.0 copy-start.4
  11.6 0.0 copy-start.5
  11.6 0.0 copy-start.6
  11.6 0.0 copy-start.7
  11.6 0.0 copy-start.8
  11.6 0.0 copy-start.9
  11.6 0.2 reshape.21
  11.8 0.3 copy.35
  12.1 0.3 reshape.22
  12.3 0.0 copy-done.10
  12.3 0.8 %broadcast_add_fusion.bias = f32[3,64,256]{2,1,0:T(8,128)} fusion(f32[3,64,256]{2,1,0:T(8,128)S(1)} %reshape.22, f32[64]{0:T(128)S(1)} %copy-done.10), kind=kLoop, calls=%fused_computation.6 | loop fusion | flops 49152 | bytes 393472 | tf_op jit(solution)/shard_map/add | solution.py:365
  13.1 0.0 copy-done.4
  13.1 0.0 copy-done.5
  13.1 0.0 copy-done.6
  13.1 0.0 copy-done.7
  13.1 0.0 copy-done.8
  13.1 0.0 copy-done.9
  13.2 0.8 %broadcast_in_dim.13.row_order = s32[384,1]{1,0:T(8,128)} reshape(s32[384]{0:T(512)S(1)} %multiply_add_fusion) | data formatting | bytes 3072 | tf_op jit(solution)/shard_map/broadcast_in_dim | solution.py:394
  14.0 0.0 collective-permute-done.1.from_west
  14.0 0.0 collective-permute-done.from_east
  14.0 0.6 copy-done.2
  14.6 0.7 copy-done.1
  15.2 18.7 %shard_map.283 = (bf16[192,1536]{1,0:T(8,128)(2,1)}, bf16[192,1536]{1,0:T(8,128)(2,1)}, bf16[256,1152]{1,0:T(8,128)(2,1)}, f32[256,384]{1,0:T(8,128)}, f32[256,1...) custom-call(bf16[14,14,384]{2,1,0:T(8,128)(2,1)} %bitcast.13, bf16[176,384]{1,0:T(8,128)(2,1)} %copy-done.1, ...), custom_call_target="tpu_custom_call" | custom-call | tf_op jit(solution)/shard_map/pallas_call | solution.py:332
  34.0 0.1 collective-permute-start.3
  34.0 2.2 %collective-permute-done.3 = bf16[192,1536]{1,0:T(8,128)(2,1)S(1)} collective-permute-done((bf16[192,1536]{1,0:T(8,128)(2,1)}, bf16[192,1536]{1,0:T(8,128)(2,1)S(1)}, u32[]{:S(2)}, u32[]{:S(2)}) %collective-permute-start.3) | collective-permute-done | bytes 589856 | tf_op jit(solution)/shard_map/ppermute | solution.py:421
  36.2 1.2 %add_convert_fusion = bf16[192,1536]{1,0:T(8,128)(2,1)S(1)} fusion(bf16[192,1536]{1,0:T(8,128)(2,1)S(1)} %collective-permute-done.3, bf16[192,1536]{1,0:T(8,128)(2,1)} %get-tuple-element.26), kind=kLoop, calls=%fused_computation | loop fusion | flops 1179648 | bytes 1769472 | tf_op jit(solution)/shard_map/convert_element_type | solution.py:424
  37.5 0.1 collective-permute-start.4
  37.5 9.0 %collective-permute-done.4 = bf16[96,1536]{1,0:T(8,128)(2,1)S(1)} collective-permute-done((bf16[96,1536]{1,0:T(8,128)(2,1)S(1)}, bf16[96,1536]{1,0:T(8,128)(2,1)S(1)}, u32[]{:S(2)}, u32[]{:S(2)}) %collective-permute-start.4) | collective-permute-done | bytes 294944 | tf_op jit(solution)/shard_map/ppermute | solution.py:421
  46.6 0.1 add_convert_fusion.1
  46.7 1.8 %collective-permute-start.5 = (bf16[48,1536]{1,0:T(8,128)(2,1)S(1)}, bf16[48,1536]{1,0:T(8,128)(2,1)S(1)}, u32[]{:S(2)}, u32[]{:S(2)}) collective-permute-start(bf16[48,1536]{1,0:T(8,128)(2,1)S(1)} %slice.43), channel_id=1, source_target_pairs={{0,2},{1,3},{2,0},{3,1},{4,6},{5,7},{6,4},{7,5},{8,10},{9,11},{10,... | collective-permute-start | bytes 442376 | tf_op jit(solution)/shard_map/ppermute | solution.py:421
  48.4 3.4 %collective-permute-done.5 = bf16[48,1536]{1,0:T(8,128)(2,1)S(1)} collective-permute-done((bf16[48,1536]{1,0:T(8,128)(2,1)S(1)}, bf16[48,1536]{1,0:T(8,128)(2,1)S(1)}, u32[]{:S(2)}, u32[]{:S(2)}) %collective-permute-start.5) | collective-permute-done | bytes 147488 | tf_op jit(solution)/shard_map/ppermute | solution.py:421
  51.9 1.0 %collective-permute-start.6 = (bf16[24,1536]{1,0:T(8,128)(2,1)S(1)}, bf16[24,1536]{1,0:T(8,128)(2,1)S(1)}, u32[]{:S(2)}, u32[]{:S(2)}) collective-permute-start(bf16[24,1536]{1,0:T(8,128)(2,1)S(1)} %slice.45), channel_id=1, source_target_pairs={{0,16},{4,20},{8,24},{12,28},{16,0},{20,4},{24,8},{28,12},{1,17},{... | collective-permute-start | bytes 221192 | tf_op jit(solution)/shard_map/ppermute | solution.py:421
  53.0 4.6 %shard_map.284 = (f32[224,384]{1,0:T(8,128)}, bf16[48,384]{1,0:T(8,128)(2,1)}, bf16[7,7,768]{2,1,0:T(8,128)(2,1)}) custom-call(bf16[256,1152]{1,0:T(8,128)(2,1)} %get-tuple-element.18.projected_grad, bf16[384,1152]{1,0:T(8,128)(2,1)} %attend_weight.3, f32[256,384]{1,0:T(8,128)} %get-tuple-element.19.normed, f32[256,1]{1,0:T(8,128)} %get-tuple-element.20.inverse_std, ...), custom_call_target="tpu_custom_call" | custom-call | tf_op jit(solution)/shard_map/pallas_call | solution.py:332
  57.6 0.6 collective-permute-start.2
  58.2 0.0 collective-permute-done.6
  58.2 1.9 %collective-permute-start.7 = (bf16[12,1536]{1,0:T(8,128)(2,1)S(1)}, bf16[12,1536]{1,0:T(8,128)(2,1)S(1)}, u32[]{:S(2)}, u32[]{:S(2)}) collective-permute-start(bf16[12,1536]{1,0:T(8,128)(2,1)S(1)} %slice.47), channel_id=1, source_target_pairs={{0,8},{4,12},{8,0},{12,4},{16,24},{20,28},{24,16},{28,20},{1,9},{5... | collective-permute-start | bytes 110600 | tf_op jit(solution)/shard_map/ppermute | solution.py:421
  60.1 4.5 %collective-permute-done.2.back = bf16[48,384]{1,0:T(8,128)(2,1)S(1)} collective-permute-done((bf16[48,384]{1,0:T(8,128)(2,1)}, bf16[48,384]{1,0:T(8,128)(2,1)S(1)}, u32[]{:S(2)}, u32[]{:S(2)}) %collective-permute-start.2) | collective-permute-done | bytes 36896 | tf_op jit(solution)/shard_map/ppermute | solution.py:431
  64.6 0.6 copy-done.3
  65.2 1.8 %shard_map.285 = bf16[14,14,384]{2,1,0:T(8,128)(2,1)} custom-call(f32[224,384]{1,0:T(8,128)} %get-tuple-element.24.part, bf16[48,384]{1,0:T(8,128)(2,1)} %copy-done.3, bf16[224,48]{1,0:T(8,128)(2,1)} %constant.86.clone.back_to_grid), custom_call_target="tpu_custom_call" | custom-call | tf_op jit(solution)/shard_map/pallas_call | solution.py:332
  67.0 0.0 collective-permute-done.7
  67.1 0.6 reshape.23
  67.7 0.6 reshape.24
  (14 shorter events, 0.2 us)
Async XLA Ops:
  0.6 8.0 %copy-start = (f32[169,12]{0,1:T(8,128)S(1)}, f32[169,12]{0,1:T(8,128)}, u32[]{:S(2)}) copy-start(f32[169,12]{0,1:T(8,128)} %param.28) | copy-start | bytes 24340
  2.6 11.4 %collective-permute-start.1 = (bf16[64,384]{1,0:T(8,128)(2,1)}, bf16[64,384]{1,0:T(8,128)(2,1)S(1)}, u32[]{:S(2)}, u32[]{:S(2)}) collective-permute-start(bf16[64,384]{1,0:T(8,128)(2,1)} %get-tuple-element.17), channel_id=1, source_target_pairs={{28,0},{0,4},{4,8},{8,12},{12,16},{16,20},{20,24},{24,28},{29,1},{... | collective-permute-start | bytes 147464 | tf_op jit(solution)/shard_map/ppermute | solution.py:431
  5.6 8.4 %collective-permute-start = (bf16[176,384]{1,0:T(8,128)(2,1)}, bf16[176,384]{1,0:T(8,128)(2,1)S(1)}, u32[]{:S(2)}, u32[]{:S(2)}) collective-permute-start(bf16[176,384]{1,0:T(8,128)(2,1)} %get-tuple-element.16), channel_id=1, source_target_pairs={{4,0},{8,4},{12,8},{16,12},{20,16},{24,20},{28,24},{0,28},{5,1},{9... | collective-permute-start | bytes 405512 | tf_op jit(solution)/shard_map/ppermute | solution.py:431
  11.6 0.8 %copy-start.10 = (f32[64]{0:T(128)S(1)}, f32[64]{0:T(128)}, u32[]{:S(2)}) copy-start(f32[64]{0:T(128)} %constant.70.clone) | copy-start | bytes 772
  11.6 1.6 %copy-start.4 = (s32[384]{0:T(512)S(1)}, s32[384]{0:T(512)}, u32[]{:S(2)}) copy-start(s32[384]{0:T(512)} %constant.82.clone) | copy-start | bytes 4612
  11.6 1.5 %copy-start.5 = (s32[384]{0:T(512)S(1)}, s32[384]{0:T(512)}, u32[]{:S(2)}) copy-start(s32[384]{0:T(512)} %constant.81.clone) | copy-start | bytes 4612
  11.6 1.5 %copy-start.6 = (s32[384]{0:T(512)S(1)}, s32[384]{0:T(512)}, u32[]{:S(2)}) copy-start(s32[384]{0:T(512)} %constant.80.clone) | copy-start | bytes 4612
  11.6 1.5 %copy-start.7 = (s32[384]{0:T(512)S(1)}, s32[384]{0:T(512)}, u32[]{:S(2)}) copy-start(s32[384]{0:T(512)} %constant.79.clone) | copy-start | bytes 4612
  11.6 1.5 %copy-start.8 = (s32[384]{0:T(512)S(1)}, s32[384]{0:T(512)}, u32[]{:S(2)}) copy-start(s32[384]{0:T(512)} %constant.78.clone) | copy-start | bytes 4612
  11.6 1.5 %copy-start.9 = (s32[384]{0:T(512)S(1)}, s32[384]{0:T(512)}, u32[]{:S(2)}) copy-start(s32[384]{0:T(512)} %constant.77.clone) | copy-start | bytes 4612
  14.0 0.6 copy-start.2
  14.6 0.7 copy-start.1
  34.0 2.3 %collective-permute-start.3 = (bf16[192,1536]{1,0:T(8,128)(2,1)}, bf16[192,1536]{1,0:T(8,128)(2,1)S(1)}, u32[]{:S(2)}, u32[]{:S(2)}) collective-permute-start(bf16[192,1536]{1,0:T(8,128)(2,1)} %get-tuple-element.27), channel_id=1, source_target_pairs={{0,1},{1,0},{2,3},{3,2},{4,5},{5,4},{6,7},{7,6},{8,9},{9,8},{10,11... | collective-permute-start | bytes 1769480 | tf_op jit(solution)/shard_map/ppermute | solution.py:421
  37.5 9.1 %collective-permute-start.4 = (bf16[96,1536]{1,0:T(8,128)(2,1)S(1)}, bf16[96,1536]{1,0:T(8,128)(2,1)S(1)}, u32[]{:S(2)}, u32[]{:S(2)}) collective-permute-start(bf16[96,1536]{1,0:T(8,128)(2,1)S(1)} %slice.41), channel_id=1, source_target_pairs={{0,4},{4,0},{8,12},{12,8},{16,20},{20,16},{24,28},{28,24},{1,5},{5... | collective-permute-start | bytes 884744 | tf_op jit(solution)/shard_map/ppermute | solution.py:421
  46.7 5.2 %collective-permute-start.5 = (bf16[48,1536]{1,0:T(8,128)(2,1)S(1)}, bf16[48,1536]{1,0:T(8,128)(2,1)S(1)}, u32[]{:S(2)}, u32[]{:S(2)}) collective-permute-start(bf16[48,1536]{1,0:T(8,128)(2,1)S(1)} %slice.43), channel_id=1, source_target_pairs={{0,2},{1,3},{2,0},{3,1},{4,6},{5,7},{6,4},{7,5},{8,10},{9,11},{10,... | collective-permute-start | bytes 442376 | tf_op jit(solution)/shard_map/ppermute | solution.py:421
  51.9 6.2 %collective-permute-start.6 = (bf16[24,1536]{1,0:T(8,128)(2,1)S(1)}, bf16[24,1536]{1,0:T(8,128)(2,1)S(1)}, u32[]{:S(2)}, u32[]{:S(2)}) collective-permute-start(bf16[24,1536]{1,0:T(8,128)(2,1)S(1)} %slice.45), channel_id=1, source_target_pairs={{0,16},{4,20},{8,24},{12,28},{16,0},{20,4},{24,8},{28,12},{1,17},{... | collective-permute-start | bytes 221192 | tf_op jit(solution)/shard_map/ppermute | solution.py:421
  57.6 7.0 %collective-permute-start.2 = (bf16[48,384]{1,0:T(8,128)(2,1)}, bf16[48,384]{1,0:T(8,128)(2,1)S(1)}, u32[]{:S(2)}, u32[]{:S(2)}) collective-permute-start(bf16[48,384]{1,0:T(8,128)(2,1)} %get-tuple-element.25), channel_id=1, source_target_pairs={{28,0},{0,4},{4,8},{8,12},{12,16},{16,20},{20,24},{24,28},{29,1},{... | collective-permute-start | bytes 110600 | tf_op jit(solution)/shard_map/ppermute | solution.py:431
  58.2 8.8 %collective-permute-start.7 = (bf16[12,1536]{1,0:T(8,128)(2,1)S(1)}, bf16[12,1536]{1,0:T(8,128)(2,1)S(1)}, u32[]{:S(2)}, u32[]{:S(2)}) collective-permute-start(bf16[12,1536]{1,0:T(8,128)(2,1)S(1)} %slice.47), channel_id=1, source_target_pairs={{0,8},{4,12},{8,0},{12,4},{16,24},{20,28},{24,16},{28,20},{1,9},{5... | collective-permute-start | bytes 110600 | tf_op jit(solution)/shard_map/ppermute | solution.py:421
  64.6 0.6 copy-start.3

commit v3 on v2

v3 whole, which is shorter than its diff:
```python
import functools

import jax
import jax.numpy as jnp
import numpy as np
from jax import lax
from jax.experimental import pallas as pl
from jax.experimental.pallas import tpu as pltpu
from jax.sharding import PartitionSpec as P

WINDOW = 7
SHIFT = 3
SLOT = 64
LANES = 128
EPS = 1e-05


def up(value, step):
    return -(-value // step) * step


def dot(left, right):
    return lax.dot_general(left, right, (((1,), (0,)), ((), ())), preferred_element_type=jnp.float32)


def dot_t(left, right):
    return lax.dot_general(left, right, (((1,), (1,)), ((), ())), preferred_element_type=jnp.float32)


def pick(select, values):
    return dot(select, values).astype(jnp.bfloat16)


class Grid:
    def __init__(self, rows, cols, heads, channels):
        self.rows, self.cols, self.heads, self.channels = rows, cols, heads, channels
        self.west = WINDOW - SHIFT
        self.last = cols - self.west
        self.bands, self.across = rows // WINDOW, cols // WINDOW
        self.windows = self.bands * self.across
        self.window_rows = self.windows * SLOT
        self.stride = up(cols, 16)
        self.own_rows = rows * self.stride
        self.west_rows = up(rows * self.west, 16)
        self.quad_lines, self.quad_cols, self.quad_west = rows // 2, cols // 2, self.west // 2
        self.quad_stride = up(self.quad_cols, 8)
        self.quad_count = up(self.quad_lines * self.quad_stride, 16)
        self.cot_stride = up(self.quad_cols, 16)
        self.cot_own = self.quad_lines * self.cot_stride
        self.cot_halo = up(self.quad_west * self.quad_lines, 16)

    def source(self, row, col):
        return row * self.stride + col if col >= 0 else self.own_rows + row * self.west + col + self.west

    def window_row(self, row, col):
        line = (row - SHIFT) % self.rows
        across, place = divmod(col + self.west, WINDOW)
        window = line // WINDOW * self.across + across
        return window * SLOT + line % WINDOW * (WINDOW + 1) + place

    def quad_row(self, row, col):
        phase = 2 * (col % 2) + row % 2
        return phase * self.quad_count + row // 2 * self.quad_stride + (col + self.west) // 2

    def onehot(self, shape, pairs):
        out = np.zeros(shape, np.float32)
        for i, j in pairs:
            out[i, j] = 1
        return jnp.asarray(out, jnp.bfloat16)

    def cells(self, first, last):
        return [(r, c) for r in range(self.rows) for c in range(first, last)]

    def to_windows(self):
        pairs = [(self.window_row(r, c), self.source(r, c)) for r, c in self.cells(-self.west, self.last)]
        return self.onehot((self.window_rows, self.own_rows + self.west_rows), pairs)

    def to_quads(self):
        pairs = [(self.quad_row(r, c), self.window_row(r, c)) for r, c in self.cells(-self.west, self.last)]
        return self.onehot((4 * self.quad_count, self.window_rows), pairs)

    def from_quads(self):
        return self.to_quads().T

    def pack_tokens(self):
        pairs = [
            (r * self.west + c - self.last, self.source(r, c)) for r, c in self.cells(self.last, self.cols)
        ]
        return self.onehot((self.west_rows, self.own_rows), pairs)

    def quad_cells(self, first, last):
        return [(i, j) for i in range(self.quad_lines) for j in range(first, last)]

    def pack_cot(self):
        first = self.quad_cols - self.quad_west
        pairs = [
            (self.quad_west * i + j - first, i * self.cot_stride + j)
            for i, j in self.quad_cells(first, self.quad_cols)
        ]
        return self.onehot((self.cot_halo, self.cot_own), pairs)

    def cot_to_quads(self):
        pairs = [
            (i * self.quad_stride + j, self.cot_own + self.quad_west * i + j)
            for i, j in self.quad_cells(0, self.quad_west)
        ]
        pairs += [
            (i * self.quad_stride + j, i * self.cot_stride + j - self.quad_west)
            for i, j in self.quad_cells(self.quad_west, self.quad_cols)
        ]
        return self.onehot((self.quad_count, self.cot_own + self.cot_halo), pairs)

    def tokens_back(self):
        pairs = [(r * self.west + c + self.west, self.window_row(r, c)) for r, c in self.cells(-self.west, 0)]
        return self.onehot((self.west_rows, self.window_rows), pairs)

    def quads_back(self):
        pairs = [
            (self.quad_west * i + j, i * self.quad_stride + j) for i, j in self.quad_cells(0, self.quad_west)
        ]
        return self.onehot((self.cot_halo, self.quad_count), pairs)

    def final_tokens(self):
        pairs = [(self.source(r, c), self.window_row(r, c)) for r, c in self.cells(0, self.last)]
        pairs += [
            (self.source(r, c), self.window_rows + r * self.west + c - self.last)
            for r, c in self.cells(self.last, self.cols)
        ]
        return self.onehot((self.own_rows, self.window_rows + self.west_rows), pairs)

    def final_quads(self):
        first = self.quad_cols - self.quad_west
        pairs = [
            (i * self.quad_stride + j, i * self.quad_stride + j + self.quad_west)
            for i, j in self.quad_cells(0, first)
        ]
        pairs += [
            (i * self.quad_stride + j, self.quad_count + self.quad_west * i + j - first)
            for i, j in self.quad_cells(first, self.quad_cols)
        ]
        return self.onehot((self.quad_count, self.quad_count + self.cot_halo), pairs)


def normalize(values):
    centred = values - jnp.mean(values, -1, keepdims=True)
    inverse_std = lax.rsqrt(jnp.mean(centred * centred, -1, keepdims=True) + EPS)
    return centred * inverse_std, inverse_std


def spread(ref, grid_ref, stride):
    ref[0 : grid_ref.shape[0] * stride, :] = jnp.zeros((grid_ref.shape[0] * stride, ref.shape[1]), ref.dtype)
    for line in range(grid_ref.shape[0]):
        ref[line * stride : line * stride + grid_ref.shape[1], :] = grid_ref[line]


def pack(grid, out, tokens, quads):
    out[0 : grid.west_rows, :] = tokens
    for part in range(quads.shape[1] // grid.channels):
        first = grid.west_rows + part * grid.cot_halo
        out[first : first + grid.cot_halo, :] = quads[:, part * grid.channels : (part + 1) * grid.channels]


def unpack(grid, ref, width):
    first = grid.west_rows
    parts = [
        ref[first + part * grid.cot_halo : first + (part + 1) * grid.cot_halo, :]
        for part in range(width // grid.channels)
    ]
    return ref[0 : grid.west_rows, :], jnp.concatenate(parts, 1)


def pre_kernel(grid, x, cot, pack_tokens, pack_cot, to_next, tokens, quads):
    spread(tokens, x.get(), grid.stride)
    spread(quads, cot.get(), grid.cot_stride)
    halo = pick(pack_cot.get()[...], quads[...])
    pack(grid, to_next.ref, pick(pack_tokens.get()[...], tokens[...]), halo)
    to_next.send()


def head_sum(stacked, head_mask, per_group):
    total = None
    for head in range(per_group):
        part = stacked[head * SLOT : (head + 1) * SLOT, :]
        part = jnp.where(head_mask[head * SLOT : (head + 1) * SLOT, :] > 0, part, 0.0)
        total = part if total is None else total + part
    return total


def main_kernel(
    grid, x, from_west, to_windows, attend_weight, head_mask, bias, mask, to_quads, output_weight, cot,
    cot_to_quads, merge_weight, from_quads, order_a, order_b,
    kept, sent, projected_grad_out, normed_out, std_out, branch_grad_out, quad16_out,
    tokens, quads, projected, attended, probs, outer,
):
    channels, heads = grid.channels, grid.heads
    head_size = channels // heads
    scale = head_size ** (-0.5)
    per_group = LANES // head_size
    groups = heads // per_group

    spread(tokens, x.get(), grid.stride)
    west_tokens, west_quads = unpack(grid, from_west.get(), quads.shape[1])
    tokens[grid.own_rows :, :] = west_tokens
    windowed = dot(to_windows.get()[...], tokens[...])
    normed, inverse_std = normalize(windowed)
    rolled = normed.astype(jnp.bfloat16)
    normed_out.ref[...] = normed
    normed_out.send()
    std_out.ref[...] = inverse_std
    std_out.send()
    projected[...] = dot(rolled, attend_weight.get()[...]).astype(jnp.bfloat16)
    mask_all = head_mask.get()[...]
    bias_ref, mask_ref = bias.get(), mask.get()

    def heads_of(rows, part, group):
        first = part * channels + group * LANES
        return projected[rows, first : first + LANES]

    def forward(window, carry):
        rows = pl.ds(pl.multiple_of(window * SLOT, SLOT), SLOT)
        extra = mask_ref[window // grid.across]
        for group in range(groups):
            lanes = group * LANES
            query, key, value = [heads_of(rows, part, group) for part in range(3)]
            spread_query = jnp.concatenate([query] * per_group, 0) * mask_all
            scores = dot_t(key, spread_query) * scale + bias_ref[group] + extra
            weights = jnp.exp(scores - jnp.max(scores, 0, keepdims=True))
            prob = weights / jnp.sum(weights, 0, keepdims=True)
            probs[window * groups + group] = prob
            mixed = dot(prob.astype(jnp.bfloat16).T, value)
            attended[rows, lanes : lanes + LANES] = head_sum(mixed, mask_all, per_group).astype(jnp.bfloat16)
        return carry

    lax.fori_loop(0, grid.windows, forward, 0)

    spread(quads, cot.get(), grid.cot_stride)
    quads[grid.cot_own :, :] = west_quads
    select = to_quads.get()[...]
    attended_quads = pick(select, attended[...])
    feature_quads = dot(select, windowed.astype(jnp.bfloat16))
    branch = dot(attended_quads, output_weight.get()[...])
    hidden = (feature_quads + branch).astype(jnp.bfloat16).astype(jnp.float32)
    count = grid.quad_count
    phases = [hidden[k * count : (k + 1) * count] for k in range(4)]
    width = 4 * channels
    mean = sum(jnp.sum(phase, -1, keepdims=True) for phase in phases) / width
    centred = [phase - mean for phase in phases]
    variance = sum(jnp.sum(phase * phase, -1, keepdims=True) for phase in centred) / width
    quad_std = lax.rsqrt(variance + EPS)
    quad_normed = [phase * quad_std for phase in centred]
    cot_quads = pick(cot_to_quads.get()[...], quads[...])
    merge_ref = merge_weight.get()
    quad_grads = []
    for k in range(4):
        quad16_out.ref[k * count : (k + 1) * count, :] = quad_normed[k].astype(jnp.bfloat16)
        quad_grads.append(dot_t(cot_quads, merge_ref[k * channels : (k + 1) * channels, :]))
    quad16_out.send()
    first = sum(jnp.sum(part, -1, keepdims=True) for part in quad_grads) / width
    second = sum(jnp.sum(part * n, -1, keepdims=True) for part, n in zip(quad_grads, quad_normed)) / width
    hidden_grad = jnp.concatenate(
        [quad_std * (part - first - n * second) for part, n in zip(quad_grads, quad_normed)], 0
    ).astype(jnp.bfloat16)
    branch_grad = pick(from_quads.get()[...], hidden_grad)
    branch_grad_out.ref[...] = branch_grad
    branch_grad_out.send()
    outer[...] = dot_t(branch_grad, output_weight.get()[...]).astype(jnp.bfloat16)
    projected_grad = projected_grad_out.ref

    def backward(window, carry):
        rows = pl.ds(pl.multiple_of(window * SLOT, SLOT), SLOT)
        for group in range(groups):
            lanes = group * LANES
            query, key, value = [heads_of(rows, part, group) for part in range(3)]
            grads = outer[rows, lanes : lanes + LANES]
            spread_query = jnp.concatenate([query] * per_group, 0) * mask_all
            spread_grads = jnp.concatenate([grads] * per_group, 0) * mask_all
            prob = probs[window * groups + group]
            value_grad = dot(prob.astype(jnp.bfloat16), spread_grads)
            score_grad = dot_t(value, spread_grads)
            inner = jnp.sum(prob * score_grad, 0, keepdims=True)
            soft = (prob * (score_grad - inner) * scale).astype(jnp.bfloat16)
            key_grad = dot(soft, spread_query)
            query_grad = head_sum(dot(soft.T, key), mask_all, per_group)
            for part, grad in enumerate((query_grad, key_grad, value_grad)):
                at = part * channels + lanes
                projected_grad[rows, at : at + LANES] = grad.astype(jnp.bfloat16)
        return carry

    lax.fori_loop(0, grid.windows, backward, 0)
    projected_grad_out.send()

    columns = lax.broadcasted_iota(jnp.int32, (channels, channels), 1)
    half, split = channels // 2, 2 * channels
    for route, ref in enumerate((order_a, order_b)):
        order = jnp.where(columns == ref.get()[...], 1.0, 0.0).astype(jnp.bfloat16)
        rolled_t = dot_t(order, rolled).astype(jnp.bfloat16)
        if route == 0:
            pieces = [(0, dot(rolled_t, projected_grad[:, :split]))]
        else:
            attended_t = dot_t(order, attended[...]).astype(jnp.bfloat16)
            pieces = [
                (split, dot(rolled_t, projected_grad[:, split:])),
                (3 * channels, dot(attended_t, branch_grad)),
            ]
        for at, piece in pieces:
            piece = piece.astype(jnp.bfloat16)
            kept.ref[:, at : at + piece.shape[1]] = piece[:half]
            sent.ref[:, at : at + piece.shape[1]] = piece[half:]
    kept.send()
    sent.send()


def tail_kernel(
    grid, projected_grad, attend_weight, normed, inverse_std, branch_grad, tokens_back, quad16, merge_weight,
    quads_back, back, feature_grads, merged,
):
    channels = grid.channels
    grads = dot_t(projected_grad.get()[...], attend_weight.get()[...])
    n = normed.get()[...]
    first = jnp.mean(grads, -1, keepdims=True)
    second = jnp.mean(grads * n, -1, keepdims=True)
    rolled_grad = inverse_std.get()[...] * (grads - first - n * second)
    total = (branch_grad.get()[...].astype(jnp.float32) + rolled_grad).astype(jnp.bfloat16)
    feature_grads.ref[...] = total
    feature_grads.send()
    count = grid.quad_count
    sums = None
    quad_ref, merge_ref = quad16.get(), merge_weight.get()
    for k in range(4):
        term = dot(quad_ref[k * count : (k + 1) * count, :], merge_ref[k * channels : (k + 1) * channels, :])
        sums = term if sums is None else sums + term
    sums = sums.astype(jnp.bfloat16)
    merged.ref[...] = sums
    merged.send()
    pack(grid, back.ref, pick(tokens_back.get()[...], total), pick(quads_back.get()[...], sums))
    back.send()


def last_kernel(grid, feature_grads, merged, came, final_tokens, final_quads, out, merged_out):
    width = merged_out.ref.shape[2]
    tokens, quads = unpack(grid, came.get(), width)
    rows = grid.window_rows
    select = final_tokens.get()
    total = dot(select[:, :rows], feature_grads.get()[...]) + dot(select[:, rows:], tokens)
    for line in range(grid.rows):
        out.ref[line] = total[line * grid.stride : line * grid.stride + grid.cols].astype(jnp.bfloat16)
    out.send()
    select = final_quads.get()
    count = grid.quad_count
    sums = dot(select[:, :count], merged.get()[...]) + dot(select[:, count:], quads)
    for line in range(grid.quad_lines):
        first = line * grid.quad_stride
        merged_out.ref[line] = sums[first : first + grid.quad_cols].astype(jnp.bfloat16)
    merged_out.send()


class Operand:
    def __init__(self, source, ref, sem):
        self.ref, self.copy, self.waited = ref, pltpu.make_async_copy(source, ref, sem), False
        self.copy.start()

    def get(self):
        if not self.waited:
            self.copy.wait()
            self.waited = True
        return self.ref


class Result:
    def __init__(self, target, ref, sem):
        self.ref, self.copy = ref, pltpu.make_async_copy(ref, target, sem)

    def send(self):
        self.copy.start()


def call(kernel, outs, *args, scratch=(), name):
    def body(*refs):
        counts = len(args), len(outs)
        given, refs = refs[: counts[0]], refs[counts[0] :]
        made, refs = refs[: counts[1]], refs[counts[1] :]
        inner, refs = refs[: len(scratch)], refs[len(scratch) :]
        buffers, sems = refs[:-1], refs[-1]
        operands = [Operand(g, buffers[i], sems.at[i]) for i, g in enumerate(given)]
        results = [
            Result(m, buffers[counts[0] + i], sems.at[counts[0] + i]) for i, m in enumerate(made)
        ]
        kernel(*operands, *results, *inner)
        for operand in operands:
            operand.get()
        for result in results:
            result.copy.wait()

    anywhere = pl.BlockSpec(memory_space=pl.ANY)
    buffers = [pltpu.VMEM(a.shape, a.dtype) for a in (*args, *outs)]
    return pl.pallas_call(
        body,
        out_shape=outs,
        in_specs=[anywhere] * len(args),
        out_specs=[anywhere] * len(outs),
        scratch_shapes=[*scratch, *buffers, pltpu.SemaphoreType.DMA((len(args) + len(outs),))],
        compiler_params=pltpu.CompilerParams(vmem_limit_bytes=56 * 2**20),
        name=name,
    )(*args)


def f32(*shape):
    return jax.ShapeDtypeStruct(shape, jnp.float32)


def b16(*shape):
    return jax.ShapeDtypeStruct(shape, jnp.bfloat16)


def window_bias(position_bias, grid):
    place = np.arange(SLOT)
    row, col = place // (WINDOW + 1), place % (WINDOW + 1)
    real = (row < WINDOW) & (col < WINDOW)
    span = 2 * WINDOW - 1
    index = (row[None, :] - row[:, None] + WINDOW - 1) * span + (col[None, :] - col[:, None] + WINDOW - 1)
    index = np.where(real[:, None] & real[None, :], index, 0)
    one_hot = jnp.asarray(index.reshape(-1)[:, None] == np.arange(span * span)[None, :]).astype(jnp.float32)
    heads = grid.heads
    values = jnp.dot(one_hot, position_bias, precision=lax.Precision.HIGHEST)
    per_group = LANES // (grid.channels // heads)
    values = values.reshape(SLOT, SLOT, heads // per_group, per_group).transpose(2, 0, 3, 1)
    values = values.reshape(heads // per_group, SLOT, per_group * SLOT)
    padded = jnp.asarray(np.where(real, 0.0, -1e30), jnp.float32)
    values = values + padded[None, :, None]
    line = np.arange(grid.bands)[:, None] * WINDOW + row[None, :]
    region = (line >= grid.rows - WINDOW).astype(int) + (line >= grid.rows - SHIFT).astype(int)
    blocked = np.where(region[:, :, None] == region[:, None, :], 0.0, -100.0)
    blocked = np.where(real[:, None] & real[None, :], blocked, 0.0)
    mask = jnp.asarray(np.concatenate([blocked] * per_group, 2), jnp.float32)
    return values, mask


def halving_bits():
    frame_bits = lax.axis_size("frame").bit_length() - 1
    azim_bits = lax.axis_size("azim").bit_length() - 1
    frame = [("frame", bit, 1 << bit) for bit in range(frame_bits)]
    azim = [("azim", bit, 1 << (bit + frame_bits)) for bit in range(azim_bits)]
    rest = frame[2:] + azim[1:]
    return [frame[:1] + azim[:1] + frame[1:2] + rest, frame[:2] + azim[:1] + rest]


def exchange(block, axis, bit):
    return lax.ppermute(block, axis, [(i, i ^ (1 << bit)) for i in range(lax.axis_size(axis))])


def row_orders(channels):
    orders = []
    for bits in halving_bits():
        members = 1 << len(bits)
        row = np.arange(channels)
        if channels % members:
            orders.append(jnp.asarray(row, jnp.int32)[:, None])
            continue
        each = channels // members
        piece = jnp.zeros(channels, jnp.int32)
        for stage, (axis, bit, weight) in enumerate(bits):
            far = (row // each >> (len(bits) - 1 - stage)) & 1
            own = (lax.axis_index(axis) >> bit) & 1
            piece = piece + (own ^ jnp.asarray(far, jnp.int32)) * weight
        orders.append((piece * each + jnp.asarray(row % each, jnp.int32))[:, None])
    return orders


def scatter_flat(terms):
    bits = halving_bits()[0]
    members = 1 << len(bits)
    widths = [term.size // members for term in terms]
    held = jnp.concatenate([term.reshape(members, -1) for term in terms], 1)
    held = held.reshape((2,) * len(bits) + (-1,))
    for axis, bit, weight in bits:
        dim = len(bits) - weight.bit_length()
        own = (lax.axis_index(axis) >> bit) & 1
        kept = lax.dynamic_slice_in_dim(held, own, 1, dim)
        got = exchange(lax.dynamic_slice_in_dim(held, 1 - own, 1, dim), axis, bit)
        total = kept.astype(jnp.float32) + got.astype(jnp.float32)
        held = total.astype(jnp.bfloat16)
    total = total.reshape(-1)
    return total[: widths[0]], total[widths[0] :]


def halve(total):
    held, half = total.astype(jnp.bfloat16), total.shape[0] // 2
    return held[:half], held[half:]


def add(kept, got):
    return kept.astype(jnp.float32) + got.astype(jnp.float32)


def scatter_sum(kept, sent, channels):
    routes = halving_bits()
    if channels % (1 << len(routes[0])):
        whole = jnp.concatenate([kept, sent], 0)
        return scatter_flat((whole[:, : 3 * channels], whole[:, 3 * channels :]))
    got = exchange(sent, *routes[0][0][:2])
    split = 2 * channels
    parts = [add(kept[:, :split], got[:, :split]), add(kept[:, split:], got[:, split:])]
    for stage in (1, 2):
        halves = [halve(part) for part in parts]
        gots = [exchange(sent, *bits[stage][:2]) for (_, sent), bits in zip(halves, routes)]
        parts = [add(kept, got) for (kept, _), got in zip(halves, gots)]
    total = jnp.concatenate(parts, 1)
    for axis, bit, _ in routes[0][3:]:
        kept, sent = halve(total)
        total = add(kept, exchange(sent, axis, bit))
    return total[:, : 3 * channels].reshape(-1), total[:, 3 * channels :].reshape(-1)


def from_behind(block, axis, distance):
    size = lax.axis_size(axis)
    return lax.ppermute(block, axis, [((i - distance) % size, i) for i in range(size)])


def per_device(features, position_bias, attend_weight, output_weight, merge_weight, cotangent):
    x, cot = features[0], cotangent[0]
    rows, cols, channels = x.shape
    heads = position_bias.shape[1]
    grid = Grid(rows, cols, heads, channels)
    width = cot.shape[2]
    bf16 = jnp.bfloat16
    halo_rows = grid.west_rows + width // channels * grid.cot_halo
    own, quads = grid.window_rows, 4 * grid.quad_count
    (to_next,) = call(
        functools.partial(pre_kernel, grid), (b16(halo_rows, channels),),
        x, cot, grid.pack_tokens(), grid.pack_cot(), name="pack",
        scratch=[pltpu.VMEM((grid.own_rows, channels), bf16), pltpu.VMEM((grid.cot_own, width), bf16)],
    )
    from_west = from_behind(to_next, "azim", 1)
    bias, mask = window_bias(position_bias, grid)
    per_group = LANES * heads // channels
    lane_head = np.arange(LANES) // (channels // heads)
    head_mask = jnp.asarray(np.repeat(np.arange(per_group), SLOT)[:, None] == lane_head[None, :]).astype(bf16)
    half = channels // 2
    kept, sent, projected_grad, normed, inverse_std, branch_grad, quad16 = call(
        functools.partial(main_kernel, grid),
        (
            b16(half, 4 * channels), b16(half, 4 * channels), b16(own, 3 * channels), f32(own, channels),
            f32(own, 1), b16(own, channels), b16(quads, channels),
        ),
        x, from_west, grid.to_windows(), attend_weight, head_mask, bias, mask, grid.to_quads(), output_weight, cot,
        grid.cot_to_quads(), merge_weight, grid.from_quads(), *row_orders(channels), name="attend",
        scratch=[
            pltpu.VMEM((grid.own_rows + grid.west_rows, channels), bf16),
            pltpu.VMEM((grid.cot_own + grid.cot_halo, width), bf16),
            pltpu.VMEM((own, 3 * channels), bf16),
            pltpu.VMEM((own, channels), bf16),
            pltpu.VMEM((grid.windows * heads // per_group, SLOT, per_group * SLOT), jnp.float32),
            pltpu.VMEM((own, channels), bf16),
        ],
    )
    back, feature_grads, merged_quads = call(
        functools.partial(tail_kernel, grid),
        (b16(halo_rows, channels), b16(own, channels), b16(grid.quad_count, width)),
        projected_grad, attend_weight, normed, inverse_std, branch_grad, grid.tokens_back(), quad16, merge_weight,
        grid.quads_back(), name="tail",
    )
    came = from_behind(back, "azim", -1)
    feature_grad, merged = call(
        functools.partial(last_kernel, grid),
        (b16(rows, cols, channels), b16(grid.quad_lines, grid.quad_cols, width)),
        feature_grads, merged_quads, came, grid.final_tokens(), grid.final_quads(), name="last",
    )
    attend_grad, output_grad = scatter_sum(kept, sent, channels)
    return (merged[None], feature_grad[None], attend_grad, output_grad)


def solution(mesh):
    in_specs = (P("frame", None, "azim", None), P(), P(), P(), P(), P("frame", None, "azim", None))
    out_specs = (
        P("frame", None, "azim", None),
        P("frame", None, "azim", None),
        P(("azim", "frame")),
        P(("azim", "frame")),
    )
    return jax.shard_map(
        per_device, mesh=mesh, in_specs=in_specs, out_specs=out_specs, check_vma=False
    )
```

time: 68.6 us -> 57.1 us (0.83)
  waiting for transfers between devices: 19.2 us -> 9.93 us
  Pallas kernels: 27.1 us -> 21.7 us
  starting transfers between devices: 11.4 us -> 14.4 us
    ppermute x5 -> x7, waiting for transfers between devices: 14.7 us -> 7.76 us  [exchange(): lax.ppermute(block, axis, [(i, i ^ 1 << bit) for i in range(lax.axis_size...]
    pallas_call x4, Pallas kernels: 27.1 us -> 21.7 us  [call(): pl.pallas_call(body, out_shape=outs, in_specs=[anywhere] * len(args), out...]
    ppermute x5 -> x7, starting transfers between devices: 4.82 us -> 8.18 us  [exchange(): lax.ppermute(block, axis, [(i, i ^ 1 << bit) for i in range(lax.axis_size...]
    ppermute x3 -> x2, waiting for transfers between devices: 4.47 us -> 2.17 us  [from_behind(): lax.ppermute(block, axis, [((i - distance) % size, i) for i in range(size)])]
    broadcast_in_dim x1 -> x2, local copies, waits for them, and re-layouts: 0.8 us -> 1.59 us  [row_orders(): orders.append((piece * each + jnp.asarray(row % each, jnp.int32))[:, None])]
    unnamed x22 -> x20, local copies, waits for them, and re-layouts: 1.94 us -> 1.32 us
    ppermute x3 -> x2, starting transfers between devices: 6.6 us -> 6.18 us  [from_behind(): lax.ppermute(block, axis, [((i - distance) % size, i) for i in range(size)])]
  transfers between devices with their start and end apart: 8 -> 9, of which waited for: 4 -> 5; matrix products, arithmetic and copies ran while one was open for 8% -> 11% of each run, Pallas kernels for 9% -> 11%
where the time goes in v3:
time: 57.1 us; the launch traced here: 56.9 us
  Pallas kernels  21.7 us (38%)
  starting transfers between devices  14.4 us (25%)
  waiting for transfers between devices  9.93 us (17%)
  local copies, waits for them, and re-layouts  4.89 us (9%)
  matrix products  2.96 us (5%)
  other arithmetic  2.13 us (4%)
  between operations  0.9 us (2%)
    pallas_call x4, Pallas kernels, call(): pl.pallas_call(body, out_shape=outs, in_specs=[anywhere] * len(args), out...  21.7 us
    ppermute x7, starting transfers between devices, exchange(): lax.ppermute(block, axis, [(i, i ^ 1 << bit) for i in range(lax.axis_size...  8.18 us
    ppermute x7, waiting for transfers between devices, exchange(): lax.ppermute(block, axis, [(i, i ^ 1 << bit) for i in range(lax.axis_size...  7.76 us
    ppermute x2, starting transfers between devices, from_behind(): lax.ppermute(block, axis, [((i - distance) % size, i) for i in range(size)])  6.18 us
    dot_general x1, matrix products, window_bias(): values = jnp.dot(one_hot, position_bias, precision=lax.Precision.HIGHEST)  2.96 us
    ppermute x2, waiting for transfers between devices, from_behind(): lax.ppermute(block, axis, [((i - distance) % size, i) for i in range(size)])  2.17 us
    broadcast_in_dim x2, local copies, waits for them, and re-layouts, row_orders(): orders.append((piece * each + jnp.asarray(row % each, jnp.int32))[:, None])  1.59 us
    unnamed x20, local copies, waits for them, and re-layouts  1.32 us
  transfers between devices with their start and end apart: 9, of which 5 were waited for; matrix products, arithmetic and copies ran while one was open for 11% of the time, Pallas kernels for 11%

profile of v3, /device:TPU:0, one launch (start us, length us, event | category | flops | bytes accessed | tf_op | source)
XLA Modules:
  0.0 56.9 jit_solution(9858954682219282210)
XLA Ops:
  0.6 0.0 copy-start
  0.6 0.0 copy-start.9
  0.7 0.0 copy-start.3
  0.7 0.0 copy-start.4
  0.7 0.0 copy-start.5
  0.7 0.0 copy-start.6
  0.7 0.0 copy-start.7
  0.7 0.0 copy-start.8
  0.7 2.0 %pack.1 = bf16[96,384]{1,0:T(8,128)(2,1)} custom-call(bf16[14,14,384]{2,1,0:T(8,128)(2,1)} %bitcast.12, bf16[7,7,768]{2,1,0:T(8,128)(2,1)} %bitcast.14, bf16[64,224]{1,0:T(8,128)(2,1)} %constant.62.clone.refs_2_, bf16[16,112]{1,0:T(8,128)(2,1)} %constant.63.clone.refs_3_), custom_call_target="tpu_custom_call" | custom-call | tf_op jit(solution)/shard_map/pack/pallas_call | solution.py:396
  2.7 3.0 %collective-permute-start = (bf16[96,384]{1,0:T(8,128)(2,1)}, bf16[96,384]{1,0:T(8,128)(2,1)S(1)}, u32[]{:S(2)}, u32[]{:S(2)}) collective-permute-start(bf16[96,384]{1,0:T(8,128)(2,1)} %pack.1), channel_id=1, source_target_pairs={{28,0},{0,4},{4,8},{8,12},{12,16},{16,20},{20,24},{24,28},{29,1},{... | collective-permute-start | bytes 221192 | tf_op jit(solution)/shard_map/ppermute | solution.py:516
  5.8 0.0 copy-done
  5.8 3.0 %fusion.11 = f32[4096,12]{0,1:T(8,128)S(1)} fusion(pred[4096,169]{1,0:T(32,128)(4,1)} %constant.64.clone, f32[169,12]{0,1:T(8,128)S(1)} %copy-done), kind=kOutput, calls=%fused_computation.28 | convolution fusion | flops 99680256 | bytes 896944 | tf_op jit(solution)/shard_map/dot_general | solution.py:424
  8.7 0.2 reshape.21
  8.9 0.3 copy.41
  9.2 0.3 reshape.22
  9.4 0.0 copy-done.9
  9.4 0.8 %broadcast_add_fusion.refs_5_ = f32[3,64,256]{2,1,0:T(8,128)} fusion(f32[3,64,256]{2,1,0:T(8,128)S(1)} %reshape.22, f32[64]{0:T(128)S(1)} %copy-done.9), kind=kLoop, calls=%fused_computation.11 | loop fusion | flops 49152 | bytes 393472 | tf_op jit(solution)/shard_map/add | solution.py:429
  10.2 0.0 copy-done.3
  10.2 0.0 copy-done.4
  10.2 0.0 copy-done.5
  10.2 0.0 copy-done.6
  10.3 0.8 %broadcast_in_dim.18.refs_14_ = s32[384,1]{1,0:T(8,128)} reshape(s32[384]{0:T(512)S(1)} %get-tuple-element.30) | data formatting | bytes 3072 | tf_op jit(solution)/shard_map/broadcast_in_dim | solution.py:465
  11.1 0.8 %broadcast_in_dim.17.refs_13_ = s32[384,1]{1,0:T(8,128)} reshape(s32[384]{0:T(512)S(1)} %get-tuple-element.31) | data formatting | bytes 3072 | tf_op jit(solution)/shard_map/broadcast_in_dim | solution.py:465
  11.8 0.0 collective-permute-done.refs_1_
  11.9 0.6 %copy-done.2 = bf16[96,384]{1,0:T(8,128)(2,1)} copy-done((bf16[96,384]{1,0:T(8,128)(2,1)}, bf16[96,384]{1,0:T(8,128)(2,1)S(1)}, u32[]{:S(2)}) %copy-start.2) | copy-done | bytes 73752
  12.5 13.3 %attend.1 = (bf16[192,1536]{1,0:T(8,128)(2,1)}, bf16[192,1536]{1,0:T(8,128)(2,1)}, bf16[256,1152]{1,0:T(8,128)(2,1)}, f32[256,384]{1,0:T(8,128)}, f32[256,1]{1,0...) custom-call(bf16[14,14,384]{2,1,0:T(8,128)(2,1)} %bitcast.13, bf16[96,384]{1,0:T(8,128)(2,1)} %copy-done.2, ...), custom_call_target="tpu_custom_call" | custom-call | tf_op jit(solution)/shard_map/attend/pallas_call | solution.py:396
  25.8 0.1 collective-permute-start.2
  25.8 2.2 %collective-permute-done.2 = bf16[192,1536]{1,0:T(8,128)(2,1)S(1)} collective-permute-done((bf16[192,1536]{1,0:T(8,128)(2,1)}, bf16[192,1536]{1,0:T(8,128)(2,1)S(1)}, u32[]{:S(2)}, u32[]{:S(2)}) %collective-permute-start.2) | collective-permute-done | bytes 589856 | tf_op jit(solution)/shard_map/ppermute | solution.py:448
  28.0 1.2 %add_convert_fusion.1 = (bf16[192,768]{1,0:T(8,128)(2,1)S(1)}, bf16[192,768]{1,0:T(8,128)(2,1)S(1)}) fusion(bf16[192,1536]{1,0:T(8,128)(2,1)S(1)} %collective-permute-done.2, bf16[192,1536]{1,0:T(8,128)(2,1)} %get-tuple-element.26), kind=kLoop, calls=%fused_computation.1 | loop fusion | flops 1179648 | bytes 1769472 | tf_op jit(solution)/shard_map/convert_element_type | solution.py:487
  29.3 1.6 %collective-permute-start.5 = (bf16[96,768]{1,0:T(8,128)(2,1)S(1)}, bf16[96,768]{1,0:T(8,128)(2,1)S(1)}, u32[]{:S(2)}, u32[]{:S(2)}) collective-permute-start(bf16[96,768]{1,0:T(8,128)(2,1)S(1)} %slice.79), channel_id=1, source_target_pairs={{0,2},{1,3},{2,0},{3,1},{4,6},{5,7},{6,4},{7,5},{8,10},{9,11},{10,... | collective-permute-start | bytes 442376 | tf_op jit(solution)/shard_map/ppermute | solution.py:448
  30.8 1.6 %collective-permute-start.3 = (bf16[96,768]{1,0:T(8,128)(2,1)S(1)}, bf16[96,768]{1,0:T(8,128)(2,1)S(1)}, u32[]{:S(2)}, u32[]{:S(2)}) collective-permute-start(bf16[96,768]{1,0:T(8,128)(2,1)S(1)} %slice.74), channel_id=1, source_target_pairs={{0,4},{4,0},{8,12},{12,8},{16,20},{20,16},{24,28},{28,24},{1,5},{5... | collective-permute-start | bytes 442376 | tf_op jit(solution)/shard_map/ppermute | solution.py:448
  32.5 2.7 %collective-permute-done.5 = bf16[96,768]{1,0:T(8,128)(2,1)S(1)} collective-permute-done((bf16[96,768]{1,0:T(8,128)(2,1)S(1)}, bf16[96,768]{1,0:T(8,128)(2,1)S(1)}, u32[]{:S(2)}, u32[]{:S(2)}) %collective-permute-start.5) | collective-permute-done | bytes 147488 | tf_op jit(solution)/shard_map/ppermute | solution.py:448
  35.3 1.6 %collective-permute-start.6 = (bf16[48,768]{1,0:T(8,128)(2,1)S(1)}, bf16[48,768]{1,0:T(8,128)(2,1)S(1)}, u32[]{:S(2)}, u32[]{:S(2)}) collective-permute-start(bf16[48,768]{1,0:T(8,128)(2,1)S(1)} %slice.81), channel_id=1, source_target_pairs={{0,4},{4,0},{8,12},{12,8},{16,20},{20,16},{24,28},{28,24},{1,5},{5... | collective-permute-start | bytes 221192 | tf_op jit(solution)/shard_map/ppermute | solution.py:448
  36.9 0.0 collective-permute-done.3
  36.9 1.6 %collective-permute-start.4 = (bf16[48,768]{1,0:T(8,128)(2,1)S(1)}, bf16[48,768]{1,0:T(8,128)(2,1)S(1)}, u32[]{:S(2)}, u32[]{:S(2)}) collective-permute-start(bf16[48,768]{1,0:T(8,128)(2,1)S(1)} %slice.76), channel_id=1, source_target_pairs={{0,2},{1,3},{2,0},{3,1},{4,6},{5,7},{6,4},{7,5},{8,10},{9,11},{10,... | collective-permute-start | bytes 221192 | tf_op jit(solution)/shard_map/ppermute | solution.py:448
  38.5 1.2 %collective-permute-done.6 = bf16[48,768]{1,0:T(8,128)(2,1)S(1)} collective-permute-done((bf16[48,768]{1,0:T(8,128)(2,1)S(1)}, bf16[48,768]{1,0:T(8,128)(2,1)S(1)}, u32[]{:S(2)}, u32[]{:S(2)}) %collective-permute-start.6) | collective-permute-done | bytes 73760 | tf_op jit(solution)/shard_map/ppermute | solution.py:448
  39.7 1.6 %collective-permute-done.4 = bf16[48,768]{1,0:T(8,128)(2,1)S(1)} collective-permute-done((bf16[48,768]{1,0:T(8,128)(2,1)S(1)}, bf16[48,768]{1,0:T(8,128)(2,1)S(1)}, u32[]{:S(2)}, u32[]{:S(2)}) %collective-permute-start.4) | collective-permute-done | bytes 73760 | tf_op jit(solution)/shard_map/ppermute | solution.py:448
  41.4 1.6 %collective-permute-start.7 = (bf16[24,1536]{1,0:T(8,128)(2,1)S(1)}, bf16[24,1536]{1,0:T(8,128)(2,1)S(1)}, u32[]{:S(2)}, u32[]{:S(2)}) collective-permute-start(bf16[24,1536]{1,0:T(8,128)(2,1)S(1)} %pad_maximum_fusion), channel_id=1, source_target_pairs={{0,8},{4,12},{8,0},{12,4},{16,24},{20,28},{24,16},{28,20},{1,9},{5... | collective-permute-start | bytes 221192 | tf_op jit(solution)/shard_map/ppermute | solution.py:448
  43.0 4.1 %tail.1 = (bf16[96,384]{1,0:T(8,128)(2,1)}, bf16[256,384]{1,0:T(8,128)(2,1)}, bf16[64,768]{1,0:T(8,128)(2,1)}) custom-call(bf16[256,1152]{1,0:T(8,128)(2,1)} %get-tuple-element.16.refs_0_, bf16[384,1152]{1,0:T(8,128)(2,1)} %refs_1_.1, f32[256,384]{1,0:T(8,128)} %get-tuple-element.17.refs_2_, f32[256,1]{1,0:T(8,128)} %get-tuple-element.18.refs_3_, ...), custom_call_target="tpu_custom_call" | custom-call | tf_op jit(solution)/shard_map/tail/pallas_call | solution.py:396
  47.1 3.2 %collective-permute-start.1 = (bf16[96,384]{1,0:T(8,128)(2,1)}, bf16[96,384]{1,0:T(8,128)(2,1)S(1)}, u32[]{:S(2)}, u32[]{:S(2)}) collective-permute-start(bf16[96,384]{1,0:T(8,128)(2,1)} %get-tuple-element.23), channel_id=1, source_target_pairs={{4,0},{8,4},{12,8},{16,12},{20,16},{24,20},{28,24},{0,28},{5,1},{9... | collective-permute-start | bytes 221192 | tf_op jit(solution)/shard_map/ppermute | solution.py:516
  50.3 0.0 collective-permute-done.7
  50.3 0.1 collective-permute-start.8
  50.4 2.2 %collective-permute-done.1.refs_2_ = bf16[96,384]{1,0:T(8,128)(2,1)S(1)} collective-permute-done((bf16[96,384]{1,0:T(8,128)(2,1)}, bf16[96,384]{1,0:T(8,128)(2,1)S(1)}, u32[]{:S(2)}, u32[]{:S(2)}) %collective-permute-start.1) | collective-permute-done | bytes 73760 | tf_op jit(solution)/shard_map/ppermute | solution.py:516
  52.6 0.6 %copy-done.1 = bf16[96,384]{1,0:T(8,128)(2,1)} copy-done((bf16[96,384]{1,0:T(8,128)(2,1)}, bf16[96,384]{1,0:T(8,128)(2,1)S(1)}, u32[]{:S(2)}) %copy-start.1) | copy-done | bytes 73752
  53.2 2.3 %last.1 = (bf16[14,14,384]{2,1,0:T(8,128)(2,1)}, bf16[7,7,768]{2,1,0:T(8,128)(2,1)}) custom-call(bf16[256,384]{1,0:T(8,128)(2,1)} %get-tuple-element.21.refs_0_, bf16[64,768]{1,0:T(8,128)(2,1)} %get-tuple-element.22.refs_1_, bf16[96,384]{1,0:T(8,128)(2,1)} %copy-done.1, bf16[224,320]{1,0:T(8,128)(2,1)} %constant.79.clone.refs_3_, ...), custom_call_target="tpu_custom_call" | custom-call | tf_op jit(solution)/shard_map/last/pallas_call | solution.py:396
  55.6 0.0 collective-permute-done.8
  55.6 0.6 %reshape.23 = f32[13824]{0:T(1024)} reshape(f32[12,1152]{1,0:T(8,128)S(1)} %slice.86) | data formatting | bytes 110592 | tf_op jit(solution)/shard_map/reshape | solution.py:511
  56.2 0.6 %reshape.24 = f32[4608]{0:T(1024)} reshape(f32[12,384]{1,0:T(8,128)S(1)} %slice.87) | data formatting | bytes 36864 | tf_op jit(solution)/shard_map/reshape | solution.py:511
  (19 shorter events, 0.2 us)
Async XLA Ops:
  0.6 5.1 %copy-start = (f32[169,12]{0,1:T(8,128)S(1)}, f32[169,12]{0,1:T(8,128)}, u32[]{:S(2)}) copy-start(f32[169,12]{0,1:T(8,128)} %param.33) | copy-start | bytes 24340
  0.6 8.8 %copy-start.9 = (f32[64]{0:T(128)S(1)}, f32[64]{0:T(128)}, u32[]{:S(2)}) copy-start(f32[64]{0:T(128)} %constant.65.clone) | copy-start | bytes 772
  0.7 9.5 %copy-start.3 = (s32[384]{0:T(512)S(1)}, s32[384]{0:T(512)}, u32[]{:S(2)}) copy-start(s32[384]{0:T(512)} %constant.76.clone) | copy-start | bytes 4612
  0.7 9.5 %copy-start.4 = (s32[384]{0:T(512)S(1)}, s32[384]{0:T(512)}, u32[]{:S(2)}) copy-start(s32[384]{0:T(512)} %constant.75.clone) | copy-start | bytes 4612
  0.7 9.5 %copy-start.5 = (s32[384]{0:T(512)S(1)}, s32[384]{0:T(512)}, u32[]{:S(2)}) copy-start(s32[384]{0:T(512)} %constant.74.clone) | copy-start | bytes 4612
  0.7 9.5 %copy-start.6 = (s32[384]{0:T(512)S(1)}, s32[384]{0:T(512)}, u32[]{:S(2)}) copy-start(s32[384]{0:T(512)} %constant.73.clone) | copy-start | bytes 4612
  0.7 9.5 %copy-start.7 = (s32[384]{0:T(512)S(1)}, s32[384]{0:T(512)}, u32[]{:S(2)}) copy-start(s32[384]{0:T(512)} %constant.72.clone) | copy-start | bytes 4612
  0.7 9.5 %copy-start.8 = (s32[384]{0:T(512)S(1)}, s32[384]{0:T(512)}, u32[]{:S(2)}) copy-start(s32[384]{0:T(512)} %constant.71.clone) | copy-start | bytes 4612
  2.7 9.1 %collective-permute-start = (bf16[96,384]{1,0:T(8,128)(2,1)}, bf16[96,384]{1,0:T(8,128)(2,1)S(1)}, u32[]{:S(2)}, u32[]{:S(2)}) collective-permute-start(bf16[96,384]{1,0:T(8,128)(2,1)} %pack.1), channel_id=1, source_target_pairs={{28,0},{0,4},{4,8},{8,12},{12,16},{16,20},{20,24},{24,28},{29,1},{... | collective-permute-start | bytes 221192 | tf_op jit(solution)/shard_map/ppermute | solution.py:516
  11.9 0.6 %copy-start.2 = (bf16[96,384]{1,0:T(8,128)(2,1)}, bf16[96,384]{1,0:T(8,128)(2,1)S(1)}, u32[]{:S(2)}) copy-start(bf16[96,384]{1,0:T(8,128)(2,1)S(1)} %collective-permute-done.refs_1_) | copy-start | bytes 221188
  25.8 2.3 %collective-permute-start.2 = (bf16[192,1536]{1,0:T(8,128)(2,1)}, bf16[192,1536]{1,0:T(8,128)(2,1)S(1)}, u32[]{:S(2)}, u32[]{:S(2)}) collective-permute-start(bf16[192,1536]{1,0:T(8,128)(2,1)} %get-tuple-element.27), channel_id=1, source_target_pairs={{0,1},{1,0},{2,3},{3,2},{4,5},{5,4},{6,7},{7,6},{8,9},{9,8},{10,11... | collective-permute-start | bytes 1769480 | tf_op jit(solution)/shard_map/ppermute | solution.py:448
  29.3 6.0 %collective-permute-start.5 = (bf16[96,768]{1,0:T(8,128)(2,1)S(1)}, bf16[96,768]{1,0:T(8,128)(2,1)S(1)}, u32[]{:S(2)}, u32[]{:S(2)}) collective-permute-start(bf16[96,768]{1,0:T(8,128)(2,1)S(1)} %slice.79), channel_id=1, source_target_pairs={{0,2},{1,3},{2,0},{3,1},{4,6},{5,7},{6,4},{7,5},{8,10},{9,11},{10,... | collective-permute-start | bytes 442376 | tf_op jit(solution)/shard_map/ppermute | solution.py:448
  30.8 6.0 %collective-permute-start.3 = (bf16[96,768]{1,0:T(8,128)(2,1)S(1)}, bf16[96,768]{1,0:T(8,128)(2,1)S(1)}, u32[]{:S(2)}, u32[]{:S(2)}) collective-permute-start(bf16[96,768]{1,0:T(8,128)(2,1)S(1)} %slice.74), channel_id=1, source_target_pairs={{0,4},{4,0},{8,12},{12,8},{16,20},{20,16},{24,28},{28,24},{1,5},{5... | collective-permute-start | bytes 442376 | tf_op jit(solution)/shard_map/ppermute | solution.py:448
  35.3 4.4 %collective-permute-start.6 = (bf16[48,768]{1,0:T(8,128)(2,1)S(1)}, bf16[48,768]{1,0:T(8,128)(2,1)S(1)}, u32[]{:S(2)}, u32[]{:S(2)}) collective-permute-start(bf16[48,768]{1,0:T(8,128)(2,1)S(1)} %slice.81), channel_id=1, source_target_pairs={{0,4},{4,0},{8,12},{12,8},{16,20},{20,16},{24,28},{28,24},{1,5},{5... | collective-permute-start | bytes 221192 | tf_op jit(solution)/shard_map/ppermute | solution.py:448
  36.9 4.4 %collective-permute-start.4 = (bf16[48,768]{1,0:T(8,128)(2,1)S(1)}, bf16[48,768]{1,0:T(8,128)(2,1)S(1)}, u32[]{:S(2)}, u32[]{:S(2)}) collective-permute-start(bf16[48,768]{1,0:T(8,128)(2,1)S(1)} %slice.76), channel_id=1, source_target_pairs={{0,2},{1,3},{2,0},{3,1},{4,6},{5,7},{6,4},{7,5},{8,10},{9,11},{10,... | collective-permute-start | bytes 221192 | tf_op jit(solution)/shard_map/ppermute | solution.py:448
  41.4 8.9 %collective-permute-start.7 = (bf16[24,1536]{1,0:T(8,128)(2,1)S(1)}, bf16[24,1536]{1,0:T(8,128)(2,1)S(1)}, u32[]{:S(2)}, u32[]{:S(2)}) collective-permute-start(bf16[24,1536]{1,0:T(8,128)(2,1)S(1)} %pad_maximum_fusion), channel_id=1, source_target_pairs={{0,8},{4,12},{8,0},{12,4},{16,24},{20,28},{24,16},{28,20},{1,9},{5... | collective-permute-start | bytes 221192 | tf_op jit(solution)/shard_map/ppermute | solution.py:448
  47.1 5.5 %collective-permute-start.1 = (bf16[96,384]{1,0:T(8,128)(2,1)}, bf16[96,384]{1,0:T(8,128)(2,1)S(1)}, u32[]{:S(2)}, u32[]{:S(2)}) collective-permute-start(bf16[96,384]{1,0:T(8,128)(2,1)} %get-tuple-element.23), channel_id=1, source_target_pairs={{4,0},{8,4},{12,8},{16,12},{20,16},{24,20},{28,24},{0,28},{5,1},{9... | collective-permute-start | bytes 221192 | tf_op jit(solution)/shard_map/ppermute | solution.py:516
  50.3 5.2 %collective-permute-start.8 = (bf16[12,1536]{1,0:T(8,128)(2,1)S(1)}, bf16[12,1536]{1,0:T(8,128)(2,1)S(1)}, u32[]{:S(2)}, u32[]{:S(2)}) collective-permute-start(bf16[12,1536]{1,0:T(8,128)(2,1)S(1)} %slice.85), channel_id=1, source_target_pairs={{0,16},{4,20},{8,24},{12,28},{16,0},{20,4},{24,8},{28,12},{1,17},{... | collective-permute-start | bytes 110600 | tf_op jit(solution)/shard_map/ppermute | solution.py:448
  52.6 0.6 %copy-start.1 = (bf16[96,384]{1,0:T(8,128)(2,1)}, bf16[96,384]{1,0:T(8,128)(2,1)S(1)}, u32[]{:S(2)}) copy-start(bf16[96,384]{1,0:T(8,128)(2,1)S(1)} %collective-permute-done.1.refs_2_) | copy-start | bytes 221188
